TPU v7x, 128 devices: a whole 4x4x4 slice. The times are simulated.
128 devices in a mesh: ctx: 16 (over y, z), ch: 8 (over x, core).
Axes of the slice: x: 4, y: 4, z: 4, core: 2. Of those that a mesh axis runs over, the one named last changes fastest.
Arguments:
- streams: bfloat16 [3, 3, 8192, 4096], P(None, None, 'ctx', 'ch'), may hold values from -6 to 6
- short_filter: float32 [3, 7, 256], P(None, None, 'ch'), may hold values from -2 to 2
- medium_filter: bfloat16 [128, 256], P(None, 'ch'), may hold values from -0.5 to 0.5
- rates: float32 [16, 256], P(None, 'ch'), as said below
- residues: float32 [16, 256], P(None, 'ch'), may hold values from -1 to 1
- cotangent: bfloat16 [3, 8192, 4096], P(None, 'ctx', 'ch'), may hold values from -60 to 60
Outputs:
- filtered: bfloat16 [3, 8192, 4096], P(None, 'ctx', 'ch')
- stream_grads: bfloat16 [3, 3, 8192, 4096], P(None, None, 'ctx', 'ch')
- short_grad: float32 [3, 7, 256], P(None, None, 'ch')
- medium_grad: float32 [128, 256], P(None, 'ch')
Inputs may be any that keep to these rules, and one draw needn't show every extreme that they name: `rates`: decay rate of each pole, between 0 and 1/30; the pole is exp(-rate).
All inputs are finite; a program needn't handle non-finite values.
Results may differ from a plain program's by a relative error of at most 0.0056.
Values may be sent and summed in bfloat16 or wider, within the bound.
A program may use at most 192 MiB of HBM per device.

v0:
```python
import jax
import jax.numpy as jnp
from jax import lax
from jax.sharding import PartitionSpec as P

GROUP = 16
SHORT = 7
MEDIUM = 128
POLES = 16


clip_norm = 100.0
highest = lax.Precision.HIGHEST


def shifted_2(block, axis, distance):
    devices = range(lax.axis_size(axis))
    route = [(i - distance, i) for i in devices if i - distance in devices]
    return lax.ppermute(block, axis, route)


def entering(part, axis, combine, identity, reverse):
    count = lax.axis_size(axis)
    place = lax.axis_index(axis)
    ahead = count - 1 - place if reverse else place
    gathered = jax.tree.map(lambda a: lax.all_gather(a, axis), part)
    state = jax.tree.map(lambda a, e: jnp.zeros_like(a) + jnp.asarray(e, a.dtype), part, identity)

    def one(step, state):
        source = count - 1 - step if reverse else step
        return combine(
            state, jax.tree.map(lambda a: lax.dynamic_index_in_dim(a, source, 0, False), gathered)
        )

    return lax.fori_loop(0, ahead, one, state)


def shortened(value):

    def short(part):
        return part.astype(jnp.bfloat16) if part.dtype == jnp.float32 else part

    return jax.tree.map(short, value)


def expand_groups(table):
    return jnp.repeat(table, GROUP, axis=-1)


def band_matrix(medium_filter):
    groups = medium_filter.shape[1]
    reverse = jnp.flip(medium_filter, 0).T
    line_vec = jnp.concatenate(
        [
            jnp.zeros((groups, 1), reverse.dtype),
            reverse,
            jnp.zeros((groups, MEDIUM), reverse.dtype),
        ],
        axis=1,
    )
    tiled = jnp.tile(line_vec, (1, MEDIUM))[:, : 2 * MEDIUM * MEDIUM]
    return tiled.reshape(groups, MEDIUM, 2 * MEDIUM)


def causal_taps(extended, short_taps, keep_rows):
    length = extended.shape[1]
    summed = jnp.zeros((extended.shape[0], keep_rows, extended.shape[2]), jnp.float32)
    for offset in range(SHORT):
        shifted = lax.slice_in_dim(extended, length - keep_rows - offset, length - offset, axis=1)
        summed = summed + short_taps[offset] * shifted.astype(jnp.float32)
    return summed


def anticausal_taps(extended, short_taps, keep_rows):
    summed = jnp.zeros((extended.shape[0], keep_rows, extended.shape[2]), jnp.float32)
    for offset in range(SHORT):
        shifted = lax.slice_in_dim(extended, offset, offset + keep_rows, axis=1)
        summed = summed + short_taps[offset] * shifted
    return summed


def split_blocks(values, block_rows):
    return values.reshape(
        values.shape[0], values.shape[1] // block_rows, block_rows, values.shape[2] // GROUP, GROUP
    )


def on_device(streams, short_filter, medium_filter, rates, residues, cotangent):
    seq_count = streams.shape[1]
    length = streams.shape[2]
    width = streams.shape[3]
    groups = width // GROUP
    block_rows = min(512, length)
    blocks = length // block_rows
    short_taps = expand_groups(short_filter)
    tail_rows = MEDIUM + SHORT - 1
    edge_rows = SHORT - 1
    head_rows = MEDIUM + SHORT - 2
    pad_rows = 2 * MEDIUM - head_rows
    prev_pair, prev_query = shifted_2(
        (streams[1:, :, length - tail_rows :], streams[0, :, length - edge_rows :]), "ctx", 1
    )
    prev_edges = (
        prev_query,
        prev_pair[0][:, tail_rows - edge_rows :],
        prev_pair[1][:, tail_rows - edge_rows :],
    )
    key_prev = causal_taps(prev_pair[0], short_taps[1], MEDIUM)
    value_prev = causal_taps(prev_pair[1], short_taps[2], MEDIUM)
    mixed_prev = (key_prev * value_prev).astype(jnp.bfloat16)
    query_ext = jnp.concatenate([prev_edges[0], streams[0]], axis=1)
    key_ext = jnp.concatenate([prev_edges[1], streams[1]], axis=1)
    value_ext = jnp.concatenate([prev_edges[2], streams[2]], axis=1)
    query = causal_taps(query_ext, short_taps[0], length)
    key_rows = causal_taps(key_ext, short_taps[1], length)
    value_rows = causal_taps(value_ext, short_taps[2], length)
    mixed_in = (key_rows * value_rows).astype(jnp.bfloat16)
    band_table = band_matrix(medium_filter)
    in_blocks = split_blocks(mixed_in, MEDIUM)
    before = jnp.concatenate([split_blocks(mixed_prev, MEDIUM), in_blocks[:, :-1]], axis=1)
    joined = jnp.concatenate([before, in_blocks], axis=2)
    mixed = jnp.einsum(
        "grs,kpsgc->kprgc", band_table, joined, preferred_element_type=jnp.float32
    ).reshape(seq_count, length, width)
    step_pos = jnp.arange(block_rows, dtype=jnp.float32)
    decay_rows = jnp.exp(-rates[None] * step_pos[:, None, None])
    growth = jnp.exp(rates[None] * step_pos[:, None, None])
    toeplitz = jnp.einsum("tng,sng->gts", residues[None] * decay_rows, growth, precision=highest)
    toeplitz = jnp.where((step_pos[:, None] >= step_pos[None, :])[None], toeplitz, 0.0)
    ahead_weight = residues[None] * decay_rows * jnp.exp(-rates)[None]
    behind_weight = residues[None] * jnp.exp(-rates[None] * (block_rows - step_pos)[:, None, None])
    end_weight = jnp.exp(-rates[None] * (block_rows - 1 - step_pos)[:, None, None])
    block_decay = jnp.exp(-rates * block_rows)[:, :, None]
    device_decay = jnp.exp(-rates * length)[:, :, None]
    gated_grad = cotangent.astype(jnp.float32) * query
    mixed_blocks = split_blocks(mixed, block_rows)
    gated_blocks = split_blocks(gated_grad, block_rows)
    long_local = jnp.einsum("gts,kbsgc->kbtgc", toeplitz, mixed_blocks, precision=highest)
    back_local = jnp.einsum("gts,kbtgc->kbsgc", toeplitz, gated_blocks, precision=highest)
    block_ends = jnp.einsum("sng,kbsgc->kbngc", end_weight, mixed_blocks, precision=highest)
    block_heads = jnp.einsum("tng,kbtgc->kbngc", decay_rows, gated_blocks, precision=highest)
    blank_state = jnp.zeros((seq_count, POLES, groups, GROUP), jnp.float32)
    running = blank_state
    block_id = 0
    starts_local = running
    running = block_decay * running + block_ends[:, block_id]
    device_end = running
    nexts_local = [blank_state] * blocks
    running = blank_state
    for block_id in reversed(range(blocks)):
        nexts_local[block_id] = running
        running = block_decay * running + block_heads[:, block_id]

    def compose(earlier, later):
        return (earlier[0] * later[0], later[0] * earlier[1] + later[1])

    neutral = (jnp.ones_like(device_decay), jnp.zeros_like(device_end))
    incoming = entering((device_decay, device_end), "ctx", compose, neutral, False)[1]
    returning = entering((device_decay, running), "ctx", compose, neutral, True)[1]
    starts_true = jnp.stack([starts_local + jnp.exp(-rates * 0)[:, :, None] * incoming], axis=1)
    long_out = (
        long_local + jnp.einsum("tng,kbngc->kbtgc", ahead_weight, starts_true, precision=highest)
    ).reshape(seq_count, length, width)
    nexts_true = jnp.stack(
        [nexts_local[0] + jnp.exp(-rates * (block_rows * (blocks - 1)))[:, :, None] * returning],
        axis=1,
    )
    mixed_grad = (
        back_local + jnp.einsum("tng,kbngc->kbtgc", behind_weight, nexts_true, precision=highest)
    ).reshape(seq_count, length, width)
    filtered = (query * long_out).astype(jnp.bfloat16)
    query_grad = cotangent.astype(jnp.float32) * long_out
    mixed_low = mixed_grad.astype(jnp.bfloat16)
    flipped = jnp.concatenate(
        [
            jnp.swapaxes(band_table[:, :, MEDIUM:], 1, 2),
            jnp.swapaxes(band_table[:, :, :MEDIUM], 1, 2),
        ],
        axis=2,
    )
    grad_blocks = split_blocks(mixed_low, MEDIUM)
    next_mixed, next_rows = shifted_2(
        (
            shortened(mixed_grad[:, :head_rows]),
            shortened(
                jnp.stack(
                    [query_grad[:, :edge_rows], key_rows[:, :edge_rows], value_rows[:, :edge_rows]]
                )
            ),
        ),
        "ctx",
        -1,
    )
    next_low = next_mixed.astype(jnp.bfloat16)
    padded_next = jnp.concatenate(
        [next_low, jnp.zeros((seq_count, pad_rows, width), jnp.bfloat16)], axis=1
    )
    next_inner = jnp.einsum(
        "grs,ksgc->krgc",
        flipped[:, :edge_rows],
        padded_next.reshape(seq_count, 2 * MEDIUM, groups, GROUP),
        preferred_element_type=jnp.float32,
    ).reshape(seq_count, edge_rows, width)
    next_grads = (next_rows[0], next_inner * next_rows[2], next_inner * next_rows[1])
    next_first = padded_next[:, :MEDIUM]
    after_blocks = jnp.concatenate([grad_blocks[:, 1:], split_blocks(next_first, MEDIUM)], axis=1)
    inner_grad = jnp.einsum(
        "grs,kpsgc->kprgc",
        flipped,
        jnp.concatenate([grad_blocks, after_blocks], axis=2),
        preferred_element_type=jnp.float32,
    ).reshape(seq_count, length, width)
    key_grad = inner_grad * value_rows
    value_grad = inner_grad * key_rows
    grads = (query_grad, key_grad, value_grad)
    exts = (query_ext, key_ext, value_ext)
    stream_grads = jnp.stack(
        [
            anticausal_taps(
                jnp.concatenate([grads[stream], next_grads[stream]], axis=1),
                short_taps[stream],
                length,
            ).astype(jnp.bfloat16)
            for stream in range(3)
        ]
    )
    short_rows = []
    for stream in range(3):
        per_offset = []
        for offset in range(SHORT):
            shifted = lax.slice_in_dim(
                exts[stream], edge_rows - offset, edge_rows - offset + length, axis=1
            )
            per_offset.append(
                jnp.sum(grads[stream] * shifted.astype(jnp.float32), axis=(0, 1))
                .reshape(groups, GROUP)
                .sum(axis=1)
            )
        short_rows.append(jnp.stack(per_offset))
    short_local = jnp.stack(short_rows)
    lag_table = jnp.einsum(
        "kprgc,kpsgc->grs", grad_blocks, joined, preferred_element_type=jnp.float32
    )
    skewed = jnp.concatenate(
        [lag_table.reshape(groups, 2 * MEDIUM * MEDIUM), jnp.zeros((groups, MEDIUM), jnp.float32)],
        axis=1,
    ).reshape(groups, MEDIUM, 2 * MEDIUM + 1)
    medium_local = jnp.flip(jnp.sum(skewed[:, :, 1 : MEDIUM + 1], axis=1), axis=1).T
    short_sum, medium_sum = lax.psum((short_local, medium_local), "ctx")
    partial_norm = jnp.sum(short_sum * short_sum) + jnp.sum(medium_sum * medium_sum)
    total_norm = jnp.sqrt(lax.psum(partial_norm, "ch"))
    factor = jnp.minimum(1.0, clip_norm / (total_norm + 1e-06))
    return (filtered, stream_grads, factor * short_sum, factor * medium_sum)


def solution(mesh):
    in_specs = (
        P(None, None, "ctx", "ch"),
        P(None, None, "ch"),
        P(None, "ch"),
        P(None, "ch"),
        P(None, "ch"),
        P(None, "ctx", "ch"),
    )
    out_specs = (
        P(None, "ctx", "ch"),
        P(None, None, "ctx", "ch"),
        P(None, None, "ch"),
        P(None, "ch"),
    )
    return jax.shard_map(
        on_device, mesh=mesh, in_specs=in_specs, out_specs=out_specs, check_vma=False
    )
```

profile of v0, /device:TPU:1, one launch (start us, length us, event | category | flops | bytes accessed | tf_op | source)
XLA Modules:
  0.0 545.2 jit_solution(7682453787839428885)
XLA Ops:
  8.2 4.4 collective-permute-start
  15.5 4.4 collective-permute-start.1
  21.3 4.6 fusion.211
  28.6 2.6 copy.85
  33.6 11.6 %convert_multiply_fusion = (f32[3,512,512]{1,2,0:T(8,128)S(1)}, f32[3,512,512]{1,2,0:T(8,128)}) fusion(bf16[3,512,512]{1,2,0:T(8,128)(2,1)} %copy.85, bf16[3,512,512]{1,2,0:T(8,128)(2,1)} %bitcast.242, bf16[3,6,512]{1,2,0:T(8,128)(2,1)} %copy-done.19, f32[512]{0:T(512)S(1)} %broadcast_in_dim.136, f32[512]{0:T(512)S(1)} %broadcast_in_dim.134, ...), kind=kLoop, calls=%fused_computation.60 | loop fusion | flops 31457280 | bytes 9469952 | tf_op jit(solution)/shard_map/mul | solution.py:135
  45.4 3.8 fusion.162
  49.1 2.3 copy.92
  51.4 13.3 %all-gather.4.cloned.1.call-start = ((), (), s32[]{:S(2)}) async-start(), calls=%async_computation | async-start | bytes 6684672 | tf_op jit(solution)/shard_map/all_gather | solution.py:26
  71.4 1.9 tile.4
  73.4 6.2 %tile.10 = bf16[32,32896]{1,0:T(8,128)(2,1)} reshape(bf16[32,128,257]{2,1,0:T(8,128)(2,1)} %tile.4) | data formatting | bytes 4210688 | tf_op jit(solution)/shard_map/tile | solution.py:61
  81.2 1.8 copy.138
  83.0 2.6 copy.135
  85.6 2.6 copy.136
  88.2 21.7 %all-gather = f32[256,32]{1,0:T(8,128)} all-gather(f32[16,32]{1,0:T(8,128)S(1)} %copy-done.76), channel_id=2, replica_groups=mesh['ctx'=16,'ch'=8] {'ctx'}, dimensions={0}, use_global_device_ids=true | all-gather | bytes 34816 | tf_op jit(solution)/shard_map/all_gather | solution.py:26
  109.9 3.1 slice_bitcast_fusion.1
  113.0 31.7 %fusion.178 = f32[32,512,512]{2,1,0:T(8,128)} fusion(f32[16,32]{0,1:T(8,128)S(1)} %copy.77, f32[16,32]{0,1:T(8,128)S(1)} %copy.76, f32[16,32]{0,1:T(8,128)S(1)} %copy.75), kind=kOutput, calls=%fused_computation.286 | convolution fusion | flops 1611399168 | bytes 33560576 | tf_op jit(solution)/shard_map/tng,sng->gts/dot_general | solution.py:128
  144.7 26.8 %fusion = f32[32,3,16,512]{3,2,1,0:T(8,128)} fusion(f32[32,512,512]{2,1,0:T(8,128)} %fusion.178, pred[512,512]{1,0:T(8,128)(4,1)S(1)} %iota_compare_fusion, f32[3,512,32,16]{1,3,2,0:T(8,128)S(1)} %bitcast.237), kind=kOutput, calls=%fused_computation.4 | convolution fusion | flops 4840226816 | bytes 40108032 | tf_op jit(solution)/shard_map/gts,kbtgc->kbsgc/dot_general | solution.py:139
  171.6 28.2 %while.27 = (s32[]{:T(128)}, f32[3,16,32,16]{2,3,1,0:T(8,128)S(1)}, s32[]{:T(128)}, f32[16,16,32,1]{2,1,3,0:T(8,128)}, f32[16,3,16,32,16]{3,4,2,1,0:T(8,128)}, /*index=5*/s32[]{:T(128)}, s32[]{:T(128)}, s32[]{:T(128)}, s32[]{:T(128)}) while((s32[]{:T(128)}, f32[3,16,32,16]{2,3,1,0:T(8,128)S(1)}, s32[]{:T(128)}, f32[16,16,32,1]{2,1,3,0:T(8,128)}, ...), condition=%wide.region_3.4_spmd, body=%wide.region_2.3_spmd.sunk | while | flops 49158 | bytes 301211 | solution.py:35
  200.3 4.4 fusion.151
  207.2 4.0 fusion.212
  211.2 2.6 copy.133
  214.7 2.3 copy.134
  217.9 3.2 multiply_convert_fusion.2
  225.6 3.0 fusion.128
  228.6 3.2 copy.101
  231.8 3.4 reshape.355
  235.3 19.1 %fusion.48 = (f32[512]{0:T(512)}, f32[512]{0:T(512)}, f32[512]{0:T(512)}, f32[512]{0:T(512)}, f32[512]{0:T(512)}, /*index=5*/f32[512]{0:T(512)}, f32[512]{0:T(512)}, f32[3,512,512]{1,2,0:T(8,128)}, f32[3,512,512]{1,2,0:T(8,128)S(1)}) fusion(bf16[3,512,512]{1,2,0:T(8,128)(2,1)} %bitcast.240, bf16[3,6,512]{1,2,0:T(8,128)(2,1)} %slice.637, ...), kind=kLoop, calls=%fused_computation.142 | loop fusion | flops 61338112 | bytes 14221312 | tf_op jit(solution)/shard_map/reduce_sum | solution.py:235
  254.4 10.4 %fusion.35 = (f32[512]{0:T(512)}, f32[512]{0:T(512)}, f32[512]{0:T(512)}, f32[512]{0:T(512)}, f32[512]{0:T(512)}, /*index=5*/f32[512]{0:T(512)}, f32[512]{0:T(512)}, f32[3,512,512]{1,2,0:T(8,128)}, f32[3,512,512]{1,2,0:T(8,128)S(1)}) fusion(bf16[3,512,512]{1,2,0:T(8,128)(2,1)S(1)} %bitcast.239, bf16[3,6,512]{1,2,0:T(8,128)(2,1)S(1)} %copy-done.15, ...), kind=kLoop, calls=%fused_computation.129 | loop fusion | flops 61338112 | bytes 14221312 | tf_op jit(solution)/shard_map/reduce_sum | solution.py:235
  272.5 2.9 fusion.159
  276.7 2.4 fusion.165
  303.4 2.1 fusion.158
  305.6 2.4 copy.140
  308.0 2.3 concatenate.55
  310.4 8.2 %reshape.380 = f32[32,128,257]{2,1,0:T(8,128)} reshape(f32[32,32896]{1,0:T(8,128)} %concatenate.55) | data formatting | bytes 8421376 | tf_op jit(solution)/shard_map/reshape | solution.py:247
  318.7 2.8 slice_reduce_fusion
  325.1 35.0 %fusion.2 = f32[32,3,16,512]{3,2,1,0:T(8,128)S(1)} fusion(f32[32,512,512]{2,1,0:T(8,128)} %fusion.178, pred[512,512]{1,0:T(8,128)(4,1)S(1)} %copy-done.18, f32[32,3,4,2,8,128]{5,4,3,2,1,0:T(8,128)} %copy-done.6), kind=kOutput, calls=%fused_computation.6 | convolution fusion | flops 4840226816 | bytes 40108032 | tf_op jit(solution)/shard_map/gts,kbsgc->kbtgc/dot_general | solution.py:138
  361.7 2.2 copy.83
  363.9 4.1 add_bitcast_fusion
  370.9 7.2 %fusion.22 = (f32[512]{0:T(512)S(1)}, f32[512]{0:T(512)S(1)}, f32[512]{0:T(512)S(1)}, f32[512]{0:T(512)S(1)}, f32[512]{0:T(512)S(1)}, /*index=5*/f32[512]{0:T(51...) fusion(bf16[3,512,512]{1,2,0:T(8,128)(2,1)S(1)} %bitcast.243, ...), kind=kLoop, calls=%fused_computation.116 | loop fusion | flops 33812992 | bytes 15761408 | tf_op jit(solution)/shard_map/reduce_sum | solution.py:235
  390.3 67.3 %all-reduce.2 = (f32[3,7,32]{2,1,0:T(8,128)S(1)}, f32[128,32]{0,1:T(8,128)S(1)}) all-reduce(f32[3,7,32]{2,1,0:T(8,128)S(1)} %pad_maximum_fusion.12, f32[128,32]{0,1:T(8,128)S(1)} %bitcast.261), channel_id=1, replica_groups=mesh['ctx'=16,'ch'=8] {'ctx'}, use_global_device_ids=true, to_apply=%region_46.47 | all-reduce | flops 4768 | bytes 38144 | tf_op jit(solution)/shard_map/psum | solution.py:249
  462.2 27.3 %psum.23 = f32[]{:T(128)} all-reduce(f32[]{:T(128)S(6)} %add.293), channel_id=1, replica_groups=mesh['ctx'=16,'ch'=8] {'ch'}, use_global_device_ids=true, to_apply=%region_51.52 | all-reduce | flops 1 | bytes 8 | tf_op jit(solution)/shard_map/psum | solution.py:251
  491.5 2.6 copy.111
  495.8 10.3 %fusion.148 = bf16[1,3,512,512]{2,3,1,0:T(8,128)(2,1)} fusion(f32[3,6,512]{1,2,0:T(8,128)S(1)} %bitcast_convert_fusion, f32[3,512,512]{1,2,0:T(8,128)S(1)} %get-tuple-element.205, f32[512]{0:T(512)S(1)} %copy-done.78, f32[512]{0:T(512)S(1)} %copy-done.80, f32[512]{0:T(512)S(1)} %copy-done.82, f32[512]{0:T(512)S(1)} %copy-done.84, f32[512]{0:T(512)} %copy-done.85, ...), kind=kLoop, calls=%fused_computation.264 | loop fusion | flops 15728640 | bytes 4769792 | tf_op jit(solution)/shard_map/stack | solution.py:217
  507.2 1.7 copy.106
  510.4 9.7 %fusion.150 = bf16[1,3,512,512]{2,3,1,0:T(8,128)(2,1)S(1)} fusion(f32[3,6,512]{1,2,0:T(8,128)S(1)} %get-tuple-element.221, f32[3,512,512]{1,2,0:T(8,128)S(1)} %copy-done.8, f32[512]{0:T(512)} %broadcast_in_dim.164, f32[512]{0:T(512)S(1)} %copy-done.48, f32[512]{0:T(512)S(1)} %copy-done.51, f32[512]{0:T(512)S(1)} %copy-done.54, f32[512]{0:T(512)} %copy-done.55, ...), kind=kLoop, calls=%fused_computation.266 | loop fusion | flops 15728640 | bytes 4769792 | tf_op jit(solution)/shard_map/stack | solution.py:217
  520.2 8.7 %fusion.149 = bf16[1,3,512,512]{2,3,1,0:T(8,128)(2,1)S(1)} fusion(f32[3,6,512]{1,2,0:T(8,128)S(1)} %get-tuple-element.220, f32[3,512,512]{1,2,0:T(8,128)S(1)} %copy-done.7, f32[512]{0:T(512)S(1)} %copy-done.58, f32[512]{0:T(512)S(1)} %copy-done.62, f32[512]{0:T(512)S(1)} %copy-done.64, f32[512]{0:T(512)S(1)} %copy-done.66, f32[512]{0:T(512)S(1)} %copy-done.68, ...), kind=kLoop, calls=%fused_computation.265 | loop fusion | flops 15728640 | bytes 4769792 | tf_op jit(solution)/shard_map/stack | solution.py:217
  528.9 2.4 pad_maximum_fusion
  531.3 6.6 %copy.112 = bf16[3,3,512,512]{3,2,1,0:T(8,128)(2,1)} copy(bf16[3,3,512,512]{2,3,1,0:T(8,128)(2,1)} %pad_maximum_fusion) | data formatting | bytes 9437184
  (391 shorter events, 117.7 us)
Async XLA Ops:
  7.2 164.4 %all-gather.6.cloned.1.call-start = ((), (), s32[]{:S(2)}) async-start(), calls=%async_computation.1 | async-start | bytes 6684672 | tf_op jit(solution)/shard_map/all_gather | solution.py:26
  8.2 24.6 %collective-permute-start = (bf16[3,6,512]{1,2,0:T(8,128)(2,1)S(1)}, bf16[3,6,512]{1,2,0:T(8,128)(2,1)S(1)}, u32[]{:S(2)}, u32[]{:S(2)}) collective-permute-start(bf16[3,6,512]{1,2,0:T(8,128)(2,1)S(1)} %bitcast.258), channel_id=1, source_target_pairs={{0,8},{8,16},{16,24},{24,32},{32,40},{40,48},{48,56},{56,64},{64,7... | collective-permute-start | bytes 55304 | tf_op jit(solution)/shard_map/ppermute | solution.py:19
  15.5 191.6 %collective-permute-start.1 = (bf16[2,3,134,512]{3,0,2,1:T(2,128)(2,1)}, bf16[2,3,134,512]{3,0,2,1:T(2,128)(2,1)}, u32[]{:S(2)}, u32[]{:S(2)}) collective-permute-start(bf16[2,3,134,512]{3,0,2,1:T(2,128)(2,1)} %copy.132), channel_id=1, source_target_pairs={{0,8},{8,16},{16,24},{24,32},{32,40},{40,48},{48,56},{56,64},{64,7... | collective-permute-start | bytes 2469896 | tf_op jit(solution)/shard_map/ppermute | solution.py:19
  21.3 123.4 %copy-start.17 = (pred[512,512]{1,0:T(8,128)(4,1)}, pred[512,512]{1,0:T(8,128)(4,1)S(1)}, u32[]{:S(2)}) copy-start(pred[512,512]{1,0:T(8,128)(4,1)S(1)} %iota_compare_fusion) | copy-start | bytes 786436
  26.7 173.1 %copy-start.27 = (f32[16,32]{1,0:T(8,128)}, f32[16,32]{1,0:T(8,128)S(1)}, u32[]{:S(2)}) copy-start(f32[16,32]{1,0:T(8,128)S(1)} %get-tuple-element.247) | copy-start | bytes 6148
  28.6 16.7 %copy-start.25 = (f32[16,32]{0,1:T(8,128)}, f32[16,32]{0,1:T(8,128)S(1)}, u32[]{:S(2)}) copy-start(f32[16,32]{0,1:T(8,128)S(1)} %copy.79) | copy-start | bytes 6148
  45.3 20.1 %copy-start.96 = (f32[32]{0:T(128)S(1)}, f32[32]{0:T(128)}, u32[]{:S(2)}) copy-start(f32[32]{0:T(128)} %get-tuple-element.225) | copy-start | bytes 388
  45.3 20.3 %copy-start.97 = (f32[32]{0:T(128)S(1)}, f32[32]{0:T(128)}, u32[]{:S(2)}) copy-start(f32[32]{0:T(128)} %get-tuple-element.244) | copy-start | bytes 388
  45.3 20.4 %copy-start.91 = (f32[16,32]{1,0:T(8,128)S(1)}, f32[16,32]{1,0:T(8,128)}, u32[]{:S(2)}) copy-start(f32[16,32]{1,0:T(8,128)} %param.14) | copy-start | bytes 6148
  45.3 20.5 %copy-start.95 = (f32[32]{0:T(128)S(1)}, f32[32]{0:T(128)}, u32[]{:S(2)}) copy-start(f32[32]{0:T(128)} %get-tuple-element.226) | copy-start | bytes 388
  45.3 20.6 %copy-start.94 = (f32[32]{0:T(128)S(1)}, f32[32]{0:T(128)}, u32[]{:S(2)}) copy-start(f32[32]{0:T(128)} %get-tuple-element.227) | copy-start | bytes 388
  45.3 20.8 %copy-start.93 = (f32[32]{0:T(128)S(1)}, f32[32]{0:T(128)}, u32[]{:S(2)}) copy-start(f32[32]{0:T(128)} %get-tuple-element.228) | copy-start | bytes 388
  51.4 308.7 %all-gather.4.cloned.1.call-start = ((), (), s32[]{:S(2)}) async-start(), calls=%async_computation | async-start | bytes 6684672 | tf_op jit(solution)/shard_map/all_gather | solution.py:26
  65.6 152.2 %copy-start.43 = (f32[512]{0:T(512)}, f32[512]{0:T(512)S(1)}, u32[]{:S(2)}) copy-start(f32[512]{0:T(512)S(1)} %broadcast_in_dim.152) | copy-start | bytes 6148
  65.7 152.0 %copy-start.46 = (f32[512]{0:T(512)}, f32[512]{0:T(512)S(1)}, u32[]{:S(2)}) copy-start(f32[512]{0:T(512)S(1)} %broadcast_in_dim.162) | copy-start | bytes 6148
  65.8 134.4 %copy-start.23 = (f32[16,32]{0,1:T(8,128)}, f32[16,32]{0,1:T(8,128)S(1)}, u32[]{:S(2)}) copy-start(f32[16,32]{0,1:T(8,128)S(1)} %copy.75) | copy-start | bytes 6148
  66.0 151.8 %copy-start.49 = (f32[512]{0:T(512)}, f32[512]{0:T(512)S(1)}, u32[]{:S(2)}) copy-start(f32[512]{0:T(512)S(1)} %broadcast_in_dim.160) | copy-start | bytes 6148
  66.1 151.7 %copy-start.52 = (f32[512]{0:T(512)}, f32[512]{0:T(512)S(1)}, u32[]{:S(2)}) copy-start(f32[512]{0:T(512)S(1)} %broadcast_in_dim.158) | copy-start | bytes 6148
  66.3 151.5 %copy-start.55 = (f32[512]{0:T(512)}, f32[512]{0:T(512)S(1)}, u32[]{:S(2)}) copy-start(f32[512]{0:T(512)S(1)} %broadcast_in_dim.156) | copy-start | bytes 6148
  66.4 151.3 %copy-start.59 = (f32[512]{0:T(512)}, f32[512]{0:T(512)S(1)}, u32[]{:S(2)}) copy-start(f32[512]{0:T(512)S(1)} %broadcast_in_dim.154) | copy-start | bytes 6148
  66.6 151.2 %copy-start.57 = (f32[512]{0:T(512)}, f32[512]{0:T(512)S(1)}, u32[]{:S(2)}) copy-start(f32[512]{0:T(512)S(1)} %broadcast_in_dim.150) | copy-start | bytes 6148
  66.8 151.1 %copy-start.61 = (f32[512]{0:T(512)}, f32[512]{0:T(512)S(1)}, u32[]{:S(2)}) copy-start(f32[512]{0:T(512)S(1)} %broadcast_in_dim.148) | copy-start | bytes 6148
  66.9 150.9 %copy-start.63 = (f32[512]{0:T(512)}, f32[512]{0:T(512)S(1)}, u32[]{:S(2)}) copy-start(f32[512]{0:T(512)S(1)} %broadcast_in_dim.146) | copy-start | bytes 6148
  67.1 150.8 %copy-start.65 = (f32[512]{0:T(512)}, f32[512]{0:T(512)S(1)}, u32[]{:S(2)}) copy-start(f32[512]{0:T(512)S(1)} %broadcast_in_dim.144) | copy-start | bytes 6148
  67.2 150.6 %copy-start.67 = (f32[512]{0:T(512)}, f32[512]{0:T(512)S(1)}, u32[]{:S(2)}) copy-start(f32[512]{0:T(512)S(1)} %broadcast_in_dim.142) | copy-start | bytes 6148
  67.4 150.5 %copy-start.69 = (f32[512]{0:T(512)}, f32[512]{0:T(512)S(1)}, u32[]{:S(2)}) copy-start(f32[512]{0:T(512)S(1)} %broadcast_in_dim.140) | copy-start | bytes 6148
  171.6 28.7 %copy-start.90 = (f32[512]{0:T(512)S(1)}, f32[512]{0:T(512)}, u32[]{:S(2)}) copy-start(f32[512]{0:T(512)} %iota_subtract_fusion) | copy-start | bytes 6148
  205.9 17.3 %collective-permute-start.3 = (bf16[3,133,512]{2,1,0:T(8,128)(2,1)}, bf16[3,133,512]{2,1,0:T(8,128)(2,1)}, u32[]{:S(2)}, u32[]{:S(2)}) collective-permute-start(bf16[3,133,512]{2,1,0:T(8,128)(2,1)} %copy.96), channel_id=1, source_target_pairs={{8,0},{16,8},{24,16},{32,24},{40,32},{48,40},{56,48},{64,56},{72,6... | collective-permute-start | bytes 1225736 | tf_op jit(solution)/shard_map/ppermute | solution.py:19
  235.2 19.2 %copy-start = (bf16[1,3,512,512]{2,3,1,0:T(8,128)(2,1)S(1)}, bf16[1,3,512,512]{2,3,1,0:T(8,128)(2,1)}, u32[]{:S(2)}) copy-start(bf16[1,3,512,512]{2,3,1,0:T(8,128)(2,1)} %copy.135) | copy-start | bytes 4718596
  235.2 19.2 %copy-start.1 = (bf16[1,3,512,512]{2,3,1,0:T(8,128)(2,1)S(1)}, bf16[1,3,512,512]{2,3,1,0:T(8,128)(2,1)}, u32[]{:S(2)}) copy-start(bf16[1,3,512,512]{2,3,1,0:T(8,128)(2,1)} %copy.136) | copy-start | bytes 4718596
  235.2 19.2 %copy-start.16 = (bf16[3,6,512]{1,2,0:T(8,128)(2,1)S(1)}, bf16[3,6,512]{1,2,0:T(8,128)(2,1)}, u32[]{:S(2)}) copy-start(bf16[3,6,512]{1,2,0:T(8,128)(2,1)} %slice.637) | copy-start | bytes 55300
  235.2 19.2 %copy-start.44 = (f32[512]{0:T(512)S(1)}, f32[512]{0:T(512)}, u32[]{:S(2)}) copy-start(f32[512]{0:T(512)} %copy-done.43) | copy-start | bytes 6148
  235.2 19.2 %copy-start.47 = (f32[512]{0:T(512)S(1)}, f32[512]{0:T(512)}, u32[]{:S(2)}) copy-start(f32[512]{0:T(512)} %copy-done.46) | copy-start | bytes 6148
  235.2 19.2 %copy-start.50 = (f32[512]{0:T(512)S(1)}, f32[512]{0:T(512)}, u32[]{:S(2)}) copy-start(f32[512]{0:T(512)} %copy-done.49) | copy-start | bytes 6148
  235.2 19.2 %copy-start.53 = (f32[512]{0:T(512)S(1)}, f32[512]{0:T(512)}, u32[]{:S(2)}) copy-start(f32[512]{0:T(512)} %copy-done.52) | copy-start | bytes 6148
  235.2 19.2 %copy-start.56 = (f32[512]{0:T(512)S(1)}, f32[512]{0:T(512)}, u32[]{:S(2)}) copy-start(f32[512]{0:T(512)} %copy-done.55) | copy-start | bytes 6148
  235.2 19.2 %copy-start.60 = (f32[512]{0:T(512)S(1)}, f32[512]{0:T(512)}, u32[]{:S(2)}) copy-start(f32[512]{0:T(512)} %copy-done.59) | copy-start | bytes 6148
  235.3 19.2 %copy-start.74 = (f32[512]{0:T(512)S(1)}, f32[512]{0:T(512)}, u32[]{:S(2)}) copy-start(f32[512]{0:T(512)} %broadcast_in_dim.164) | copy-start | bytes 6148
  279.1 24.4 %copy-start.12 = (bf16[3,4,128,32,16]{2,1,4,0,3:T(4,128)(2,1)S(1)}, bf16[3,4,128,32,16]{2,1,4,0,3:T(4,128)(2,1)}, u32[]{:S(2)}) copy-start(bf16[3,4,128,32,16]{2,1,4,0,3:T(4,128)(2,1)} %copy-done.11) | copy-start | bytes 4718596
  310.4 13.2 %copy-start.41 = (f32[32,16]{1,0:T(8,128)S(1)}, f32[32,16]{1,0:T(8,128)}, u32[]{:S(2)}) copy-start(f32[32,16]{1,0:T(8,128)} %reshape.366) | copy-start | bytes 6148
  310.4 13.4 %copy-start.42 = (f32[32,16]{1,0:T(8,128)S(1)}, f32[32,16]{1,0:T(8,128)}, u32[]{:S(2)}) copy-start(f32[32,16]{1,0:T(8,128)} %reshape.365) | copy-start | bytes 6148
  310.4 14.7 %copy-start.18 = (pred[512,512]{1,0:T(8,128)(4,1)S(1)}, pred[512,512]{1,0:T(8,128)(4,1)}, u32[]{:S(2)}) copy-start(pred[512,512]{1,0:T(8,128)(4,1)} %copy-done.17) | copy-start | bytes 786436
  370.9 19.4 %copy-start.28 = (f32[32,128]{1,0:T(8,128)S(1)}, f32[32,128]{1,0:T(8,128)}, u32[]{:S(2)}) copy-start(f32[32,128]{1,0:T(8,128)} %rev.9) | copy-start | bytes 49156
  457.6 38.1 %copy-start.78 = (f32[512]{0:T(512)S(1)}, f32[512]{0:T(512)}, u32[]{:S(2)}) copy-start(f32[512]{0:T(512)} %copy-done.77) | copy-start | bytes 6148
  457.6 38.1 %copy-start.80 = (f32[512]{0:T(512)S(1)}, f32[512]{0:T(512)}, u32[]{:S(2)}) copy-start(f32[512]{0:T(512)} %copy-done.79) | copy-start | bytes 6148
  457.6 38.1 %copy-start.82 = (f32[512]{0:T(512)S(1)}, f32[512]{0:T(512)}, u32[]{:S(2)}) copy-start(f32[512]{0:T(512)} %copy-done.81) | copy-start | bytes 6148
  457.6 38.1 %copy-start.84 = (f32[512]{0:T(512)S(1)}, f32[512]{0:T(512)}, u32[]{:S(2)}) copy-start(f32[512]{0:T(512)} %copy-done.83) | copy-start | bytes 6148
  460.9 33.1 %collective-permute-start.2 = (bf16[3,3,6,512]{3,2,1,0:T(8,128)(2,1)S(1)}, bf16[3,3,6,512]{3,2,1,0:T(8,128)(2,1)S(1)}, u32[]{:S(2)}, u32[]{:S(2)}) collective-permute-start(bf16[3,3,6,512]{3,2,1,0:T(8,128)(2,1)S(1)} %pad_maximum_fusion.11), channel_id=1, source_target_pairs={{8,0},{16,8},{24,16},{32,24},{40,32},{48,40},{56,48},{64,56},{72,6... | collective-permute-start | bytes 165896 | tf_op jit(solution)/shard_map/ppermute | solution.py:19
  (58 other events, 391.5 us)
Sparse Core Ops, SparseCore 0:
  51.5 61.7 all-gather.5
  276.8 63.9 all-gather.3
where the time goes:
time: 556 us; the launch traced here: 545 us
  local copies, waits for them, and re-layouts  149 us (27%)
  other arithmetic  120 us (22%)
  matrix products  117 us (21%)
  blocking collectives  116 us (21%)
  starting transfers between devices  24.8 us (4%)
  between operations  17.8 us (3%)
    psum x1, blocking collectives, on_device(): short_sum, medium_sum = lax.psum((short_local, medium_local), 'ctx')  67.3 us
    unnamed x210, local copies, waits for them, and re-layouts  38.7 us
    reduce_sum x3, other arithmetic, on_device(): jnp.sum(grads[stream] * shifted.astype(jnp.float32), axis=(0, 1))  36.6 us
    dot_general x1, matrix products, on_device(): jnp.einsum('gts,kbsgc->kbtgc', toeplitz, mixed_blocks, precision=highest)  35 us
    dot_general x1, matrix products, on_device(): jnp.einsum('tng,sng->gts', residues[None] * decay_rows, growth, precision...  31.7 us
    another operation x4, other arithmetic, on_device(): jnp.stack([anticausal_taps(jnp.concatenate([grads[stream], next_grads[str...  31.1 us
    psum x1, blocking collectives, on_device(): total_norm = jnp.sqrt(lax.psum(partial_norm, 'ch'))  27.3 us
    dot_general x1, matrix products, on_device(): jnp.einsum('gts,kbtgc->kbsgc', toeplitz, gated_blocks, precision=highest)  26.8 us
  transfers between devices with their start and end apart: 6, of which 0 were waited for; matrix products, arithmetic and copies ran while one was open for 46% of the time, Pallas kernels for 0%

commit v1 on v0

v1 whole, which is shorter than its diff:
```python
import functools

import jax
import jax.numpy as jnp
from jax import lax
from jax.experimental import pallas as pl
from jax.experimental.pallas import tpu as pltpu
from jax.sharding import PartitionSpec as P

GROUP = 16
SHORT = 7
MEDIUM = 128
POLES = 16
LANES = 128
HALO = 8
MESH = pl.DeviceIdType.MESH
VMEM_LIMIT = 58 * 1024 * 1024

clip_norm = 100.0
highest = lax.Precision.HIGHEST
f32 = jnp.float32
bf16 = jnp.bfloat16
NN = (((1,), (0,)), ((), ()))
NT = (((1,), (1,)), ((), ()))


def matmul(a, b, dims=NN, precision=None):
    return lax.dot_general(a, b, dims, precision=precision, preferred_element_type=f32)


def group_mask(shape, row_unit, lane_unit):
    rows = lax.broadcasted_iota(jnp.int32, shape, 0) // row_unit
    lanes = lax.broadcasted_iota(jnp.int32, shape, 1) // lane_unit
    return rows == lanes


def fill_rows(rows_ref, stream_ref, prev_ref, index):
    rows_ref[index, :HALO] = prev_ref[index, 0].astype(f32)
    rows_ref[index, HALO:] = stream_ref[index, 0].astype(f32)


def front_kernel(stream_ref, prev_ref, tap_ref, cot_ref, rate_ref, short_ref, u_ref, e_ref, state_ref, rows_ref, weight_ref):
    seq = pl.program_id(1)
    length = stream_ref.shape[2]
    block = 64

    @pl.when(seq == 0)
    def _():
        step = lax.broadcasted_iota(jnp.int32, (LANES, length), 1).astype(f32)
        rate = rate_ref[...]
        for way in range(2):
            back = (length - 1.0) - step if way == 0 else step
            full = jnp.exp(-rate * back)
            high = full.astype(bf16)
            weight_ref[way, 0] = high
            weight_ref[way, 1] = (full - high.astype(f32)).astype(bf16)

    for stream in range(3):
        fill_rows(rows_ref, stream_ref, prev_ref, stream)
    u_parts = []
    e_parts = []
    for first in range(0, length, block):
        sums = []
        for stream in range(3):
            total = None
            for offset in range(SHORT):
                begin = first + HALO - offset
                term = tap_ref[stream, offset : offset + 1, :] * rows_ref[stream, begin : begin + block, :]
                total = term if total is None else total + term
            short_ref[stream, 0, first : first + block, :] = total
            sums.append(total)
        u_parts.append((sums[1] * sums[2]).astype(bf16))
        e_parts.append((cot_ref[0, first : first + block, :].astype(f32) * sums[0]).astype(bf16))
    u = jnp.concatenate(u_parts, axis=0)
    e = jnp.concatenate(e_parts, axis=0)
    u_ref[:, 0] = u.T.reshape(LANES // GROUP, GROUP, length)
    e_ref[:, 0] = e.T.reshape(LANES // GROUP, GROUP, length)
    mask = group_mask((LANES, LANES), POLES, GROUP)
    for way, value in ((0, u), (1, e)):
        every = matmul(weight_ref[way, 0], value) + matmul(weight_ref[way, 1], value)
        own = jnp.where(mask, every, 0.0).reshape(LANES // POLES, POLES, LANES).sum(axis=0)
        row = pl.multiple_of(way * 3 * POLES + seq * POLES, POLES)
        state_ref[0, pl.ds(row, POLES), :] = own


def exchange_kernel(count, state_ref, decay_ref, u_ref, e_ref, out_ref, u_halo_ref, e_halo_ref, got, scan, back, sems, halo_sems):
    me = lax.axis_index("ctx")
    after = lax.rem(me + 1, count)
    before = lax.rem(me + count - 1, count)
    barrier = pltpu.get_barrier_semaphore()
    for step in range(1, count):
        pl.semaphore_signal(barrier, inc=1, device_id={"ctx": lax.rem(me + step, count)}, device_id_type=MESH)
    pl.semaphore_wait(barrier, count - 1)
    length = u_ref.shape[3]

    def phase(source, target, first):
        copies = []
        for step in range(1, count):
            peer = lax.rem(me + step, count)
            copies.append(
                pltpu.make_async_remote_copy(
                    src_ref=source.at[peer],
                    dst_ref=target.at[me],
                    send_sem=sems.at[first, peer],
                    recv_sem=sems.at[first + 1, me],
                    device_id={"ctx": peer},
                    device_id_type=MESH,
                )
            )
        return copies

    def arrivals(source, target, first):
        for step in range(1, count):
            peer = lax.rem(me + step, count)
            pltpu.make_async_remote_copy(
                src_ref=source.at[peer],
                dst_ref=target.at[peer],
                send_sem=sems.at[first, peer],
                recv_sem=sems.at[first + 1, peer],
                device_id={"ctx": peer},
                device_id_type=MESH,
            ).wait_recv()

    sends = phase(state_ref, got, 0)
    for copy in sends:
        copy.start()
    halos = [
        pltpu.make_async_remote_copy(
            src_ref=u_ref.at[:, :, :, pl.ds(length - LANES, LANES)],
            dst_ref=u_halo_ref,
            send_sem=halo_sems.at[0],
            recv_sem=halo_sems.at[1],
            device_id={"ctx": after},
            device_id_type=MESH,
        ),
        pltpu.make_async_remote_copy(
            src_ref=e_ref.at[:, :, :, pl.ds(0, LANES)],
            dst_ref=e_halo_ref,
            send_sem=halo_sems.at[2],
            recv_sem=halo_sems.at[3],
            device_id={"ctx": before},
            device_id_type=MESH,
        ),
    ]
    for copy in halos:
        copy.start()
    got[pl.ds(me, 1)] = state_ref[pl.ds(me, 1)]
    decay = decay_ref[pl.ds(me, 1)][0]
    arrivals(state_ref, got, 0)
    forward = lax.rem(me, 4) < 2
    running = jnp.zeros_like(decay)
    ahead = []
    for source in range(count):
        ahead.append(running)
        running = decay * running + got[source]
    running = jnp.zeros_like(decay)
    behind = [None] * count
    for source in reversed(range(count)):
        behind[source] = running
        running = decay * running + got[source]
    for target in range(count):
        scan[target] = jnp.where(forward, ahead[target], behind[target])
    returns = phase(scan, back, 2)
    for copy in returns:
        copy.start()
    back[pl.ds(me, 1)] = scan[pl.ds(me, 1)]
    arrivals(scan, back, 2)
    out_ref[...] = back[...]
    for copy in sends + returns:
        copy.wait_send()
    for copy in halos:
        copy.wait()


def slanted(row, length):
    wide = jnp.broadcast_to(row, (LANES, length))
    return pltpu.roll(wide, 0, 1, stride=1, stride_axis=0).astype(bf16)


def long_kernel(edge_ref, u_ref, u_halo_ref, e_ref, e_halo_ref, carry_ref, rate_ref, residue_ref, tap_ref, back_tap_ref,
                s_ref, w_ref, lag_ref, turned_ref):
    length = u_ref.shape[3]
    half = length // 2
    per_step = u_ref.shape[0]
    rows = 3 * GROUP
    has_prev = edge_ref[0] > 0
    has_next = edge_ref[1] > 0
    turned_ref[...] = carry_ref[0].T
    mask = group_mask((rows, 3 * POLES), GROUP, POLES)

    def one(index):
        rate = rate_ref[index]
        residue = residue_ref[index]
        first = pl.multiple_of(index * GROUP, GROUP)
        carry = turned_ref[pl.ds(first, GROUP), :]
        ahead = jnp.concatenate([carry[:, : 3 * POLES]] * 3, axis=0)
        behind = jnp.concatenate([carry[:, 3 * POLES :]] * 3, axis=0)
        u_halo = jnp.where(has_prev, u_halo_ref[index].reshape(rows, LANES), jnp.zeros((), bf16))
        e_halo = jnp.where(has_next, e_halo_ref[index].reshape(rows, LANES), jnp.zeros((), bf16))
        u_own = u_ref[index].reshape(rows, length)
        e_own = e_ref[index].reshape(rows, length)
        u_ext = jnp.concatenate([u_halo, u_own], axis=1)

        def lanes(shape):
            return lax.broadcasted_iota(jnp.int32, shape, 1).astype(f32)

        edge = lanes((POLES, LANES))

        def local_state(value, back):
            full = jnp.exp(-rate * back)
            high = full.astype(bf16)
            low = (full - high.astype(f32)).astype(bf16)
            high = jnp.concatenate([high] * 3, axis=0)
            low = jnp.concatenate([low] * 3, axis=0)
            return matmul(value, high, NT) + matmul(value, low, NT)

        ahead_far = jnp.where(mask, ahead - local_state(u_halo, (LANES - 1.0) - edge), 0.0)
        behind_near = jnp.where(mask, behind, 0.0)
        behind_far = jnp.where(mask, behind - local_state(e_halo, edge), 0.0)

        back_lag = 512.0 + 0.0 * lanes((POLES, 6 * LANES)) - lanes((POLES, 6 * LANES))
        h_back = jnp.sum(jnp.where(back_lag >= 0, residue * jnp.exp(-rate * jnp.maximum(back_lag, 0.0)), 0.0), axis=0, keepdims=True)
        lag = lanes((POLES, 6 * LANES)) - LANES
        h_ahead = jnp.sum(jnp.where(lag >= 0, residue * jnp.exp(-rate * jnp.maximum(lag, 0.0)), 0.0), axis=0, keepdims=True)
        taps = tap_ref[index]
        q = matmul(jnp.broadcast_to(taps, (16, LANES)).astype(bf16), slanted(h_ahead, 6 * LANES))[:1]
        q = jnp.where(lax.broadcasted_iota(jnp.int32, q.shape, 1) >= LANES, q, 0.0)
        q = jnp.concatenate([q, jnp.zeros((1, LANES), f32)], axis=1)
        q_table = slanted(q, 7 * LANES)
        h_table = slanted(h_back, 6 * LANES)
        k_table = slanted(back_tap_ref[index], 4 * LANES)

        moment = jnp.sum(taps * jnp.exp(rate * edge), axis=1, keepdims=True)
        time = lanes((POLES, length))
        ahead_weight = residue * moment * jnp.exp(-rate * (time + 1.0))
        ahead_weight = jnp.concatenate([ahead_weight] * 3, axis=0)
        wide = lanes((POLES, length + LANES))
        behind_weight = residue * jnp.exp(rate * (wide - length))
        behind_weight = jnp.concatenate([behind_weight] * 3, axis=0)

        left = jnp.concatenate(
            [
                jnp.concatenate([jnp.zeros((rows, half), bf16), u_ext[:, : 3 * LANES]], axis=1),
                u_ext,
            ],
            axis=0,
        )
        right = jnp.concatenate([q_table[:, 512 - LANES * b : 768 - LANES * b] for b in range(5)], axis=0)
        s_local = matmul(left, right)
        s_far = matmul(ahead_far, ahead_weight, precision=highest)
        s_ref[index] = (jnp.concatenate([s_local[:rows], s_local[rows:]], axis=1) + s_far).reshape(3, GROUP, length)

        left = jnp.concatenate(
            [
                e_own,
                jnp.concatenate([e_own[:, half:], jnp.zeros((rows, half), bf16)], axis=1),
                jnp.concatenate([e_halo, jnp.zeros((rows, length - LANES), bf16)], axis=1),
            ],
            axis=0,
        )
        right = jnp.concatenate([h_table[:, 512 - LANES * b : 768 - LANES * b] for b in range(4)], axis=0)
        p_local = matmul(left, right)
        p_local = jnp.concatenate([p_local[:rows], p_local[rows : 2 * rows], p_local[2 * rows :, :LANES]], axis=1)
        p_near = matmul(behind_near, behind_weight[:, :length], precision=highest)
        p_far = matmul(behind_far, behind_weight[:, length:], precision=highest)
        p = (p_local + jnp.concatenate([p_near, p_far], axis=1)).astype(bf16)
        p_next = jnp.where(has_next, p[:, length:], jnp.zeros((), bf16))
        p = jnp.concatenate([p[:, :length], p_next], axis=1)

        left = jnp.concatenate([p[:, : 3 * LANES], p[:, half:]], axis=0)
        right = jnp.concatenate([k_table[:, 256 - LANES * b : 512 - LANES * b] for b in range(3)], axis=0)
        w = matmul(left, right)
        w_ref[index] = jnp.concatenate([w[:rows], w[rows:]], axis=1).reshape(3, GROUP, length)

        p_stack = jnp.concatenate([p[:, LANES * b : LANES * (b + 1)] for b in range(4)], axis=0)
        u_stack = jnp.concatenate([u_ext[:, LANES * b : LANES * (b + 2)] for b in range(4)], axis=0)
        table = matmul(p_stack.T, u_stack)
        total = table[LANES - 8 :]
        for tile in reversed(range(LANES // 8 - 1)):
            total = pltpu.roll(total, 2 * LANES - 8, 1) + table[8 * tile : 8 * tile + 8]
        sub = lax.broadcasted_iota(jnp.int32, total.shape, 0)
        for bit in (1, 2, 4):
            total = jnp.where((sub & bit) > 0, pltpu.roll(total, 2 * LANES - bit, 1), total)
        total = jnp.sum(total, axis=0, keepdims=True)
        lag_ref[index] = pltpu.roll(total, 2 * LANES - 1, 1)[:, :LANES]

    def body(step, carry):
        one(2 * step)
        one(2 * step + 1)
        return carry

    lax.fori_loop(0, per_step // 2, body, 0)


def back_kernel(short_ref, stream_ref, prev_ref, tap_ref, cot_ref, s_ref, w_ref, out_ref, grad_ref, head_ref, tail_ref, corr_ref,
                rows_ref, g_ref, s_rows, w_rows, acc_ref):
    chunk = pl.program_id(0)
    seq = pl.program_id(1)
    length = stream_ref.shape[2]
    block = 64

    @pl.when(seq == 0)
    def _():
        acc_ref[...] = jnp.zeros_like(acc_ref)

    for stream in range(3):
        fill_rows(rows_ref, stream_ref, prev_ref, stream)
        g_ref[stream, length:] = jnp.zeros((HALO, LANES), f32)
    s_rows[...] = s_ref[:, 0].reshape(LANES, length).T
    w_rows[...] = w_ref[:, 0].reshape(LANES, length).T
    for first in range(0, length, block):
        here = slice(first, first + block)
        s = s_rows[here]
        w = w_rows[here]
        cot = cot_ref[0, here].astype(f32)
        out_ref[0, here] = (short_ref[0, 0, here] * s).astype(bf16)
        g_ref[0, here] = cot * s
        g_ref[1, here] = w * short_ref[2, 0, here]
        g_ref[2, here] = w * short_ref[1, 0, here]
    for stream in range(3):
        head_ref[stream, 0] = g_ref[stream, :HALO]
        for first in range(0, length, block):
            total = None
            own = g_ref[stream, first : first + block]
            for offset in range(SHORT):
                term = tap_ref[stream, offset : offset + 1, :] * g_ref[stream, first + offset : first + offset + block]
                total = term if total is None else total + term
                begin = first + HALO - offset
                part = (own * rows_ref[stream, begin : begin + block]).reshape(block // 8, 8, LANES).sum(axis=0)
                acc_ref[stream, offset] += part
            grad_ref[stream, 0, first : first + block] = total.astype(bf16)
            if first + block == length:
                tail_ref[stream, 0] = total[block - HALO :]

    @pl.when(seq == pl.num_programs(1) - 1)
    def _():
        lane = lax.broadcasted_iota(jnp.int32, (LANES, LANES), 0) // GROUP + chunk * (LANES // GROUP)
        pick = jnp.where(lane == lax.broadcasted_iota(jnp.int32, (LANES, LANES), 1), 1.0, 0.0)
        sums = acc_ref[...].sum(axis=2).reshape(3 * 8, LANES)
        value = matmul(sums, pick, precision=highest)

        @pl.when(chunk == 0)
        def _():
            corr_ref[...] = value

        @pl.when(chunk > 0)
        def _():
            corr_ref[...] += value


def reduce_kernel(count, across, corr_ref, lag_ref, head_ref, corr_out, lag_out, head_out, mine, got, norm_mine, norm_got, sems, norm_sems, head_sems):
    me = lax.axis_index("ctx")
    col = lax.axis_index("ch")
    before = lax.rem(me + count - 1, count)
    barrier = pltpu.get_barrier_semaphore()
    for step in range(1, count):
        pl.semaphore_signal(barrier, inc=1, device_id={"ctx": lax.rem(me + step, count)}, device_id_type=MESH)
    for step in range(1, across):
        pl.semaphore_signal(barrier, inc=1, device_id={"ch": lax.rem(col + step, across)}, device_id_type=MESH)
    pl.semaphore_wait(barrier, count + across - 2)
    top = corr_ref.shape[0]
    mine[:top] = corr_ref[...]
    mine[top:] = lag_ref[...]

    def send(source, target, pair, axis, here, peer):
        return pltpu.make_async_remote_copy(
            src_ref=source,
            dst_ref=target.at[here],
            send_sem=pair.at[0, peer],
            recv_sem=pair.at[1, here],
            device_id={axis: peer},
            device_id_type=MESH,
        )

    copies = []
    for step in range(1, count):
        copies.append(send(mine, got, sems, "ctx", me, lax.rem(me + step, count)))
    for copy in copies:
        copy.start()
    head = pltpu.make_async_remote_copy(
        src_ref=head_ref,
        dst_ref=head_out,
        send_sem=head_sems.at[0],
        recv_sem=head_sems.at[1],
        device_id={"ctx": before},
        device_id_type=MESH,
    )
    head.start()
    got[pl.ds(me, 1)] = mine[...][None]
    for step in range(1, count):
        peer = lax.rem(me + step, count)
        send(mine, got, sems, "ctx", peer, peer).wait_recv()
    total = got[0]
    for source in range(1, count):
        total = total + got[source]
    rows = jnp.sum((total * total).reshape(total.shape[0] // 8, 8, LANES), axis=0)
    norm_mine[...] = rows
    norms = []
    for step in range(1, across):
        norms.append(send(norm_mine, norm_got, norm_sems, "ch", col, lax.rem(col + step, across)))
    for copy in norms:
        copy.start()
    norm_got[pl.ds(col, 1)] = rows[None]
    for step in range(1, across):
        peer = lax.rem(col + step, across)
        send(norm_mine, norm_got, norm_sems, "ch", peer, peer).wait_recv()
    squares = norm_got[0]
    for source in range(1, across):
        squares = squares + norm_got[source]
    norm = jnp.sqrt(jnp.sum(jnp.sum(squares, axis=1, keepdims=True), axis=0, keepdims=True))
    factor = jnp.minimum(1.0, clip_norm / (norm + 1e-06))
    corr_out[...] = total[:top] * factor
    lag_out[...] = total[top:] * factor
    for copy in copies + norms:
        copy.wait_send()
    head.wait()


def edge_kernel(edge_ref, grad_ref, tail_ref, head_ref, tap_ref, out_ref):
    has_next = edge_ref[1] > 0
    out_ref[...] = grad_ref[...]
    for stream in range(3):
        for seq in range(3):
            head = jnp.where(has_next, head_ref[stream, seq], 0.0)
            wide = jnp.concatenate([jnp.zeros((HALO, head.shape[1]), f32), head], axis=0)
            total = tail_ref[stream, seq]
            for offset in range(1, SHORT):
                total = total + tap_ref[stream, offset : offset + 1, :] * wide[offset : offset + HALO]
            low = jnp.concatenate([jnp.zeros_like(total), total], axis=0).astype(bf16)
            keep = lax.broadcasted_iota(jnp.int32, low.shape, 0) < HALO
            out_ref[stream, seq] = jnp.where(keep, grad_ref[stream, seq], low)


def params(**more):
    return pltpu.CompilerParams(vmem_limit_bytes=VMEM_LIMIT, **more)


def on_device(streams, short_filter, medium_filter, rates, residues, cotangent):
    count = lax.axis_size("ctx")
    across = lax.axis_size("ch")
    place = lax.axis_index("ctx")
    seqs, length, width = streams.shape[1:]
    groups = width // GROUP
    chunks = width // LANES
    per_chunk = LANES // GROUP
    shape = jax.ShapeDtypeStruct

    prev = lax.ppermute(streams[:, :, length - HALO :], "ctx", [(i - 1, i) for i in range(1, count)])
    taps = jnp.pad(jnp.repeat(short_filter, GROUP, axis=-1), ((0, 0), (0, 8 - SHORT), (0, 0)))
    rate_rows = rates.T
    rate_cols = rate_rows[:, :, None]
    residue_cols = residues.T[:, :, None]
    medium = medium_filter.astype(f32).T
    tap_rows = medium[:, None, :]
    back_taps = jnp.pad(jnp.flip(medium, 1), ((0, 0), (MEDIUM + 1, 2 * MEDIUM - 1)))[:, None, :]
    edges = jnp.stack([place, count - 1 - place]).astype(jnp.int32)
    decay = jnp.repeat(jnp.exp(-rates * length), GROUP, axis=-1)
    decay = jnp.tile(decay.reshape(POLES, chunks, LANES).transpose(1, 0, 2), (1, 2 * seqs, 1))

    chunk_block = lambda c, k: (0, k, 0, c)
    turned_block = lambda c, k: (c, k, 0, 0)
    stream_spec = pl.BlockSpec((3, 1, length, LANES), chunk_block)
    prev_spec = pl.BlockSpec((3, 1, HALO, LANES), chunk_block)
    tap_spec = pl.BlockSpec((3, 8, LANES), lambda c, k: (0, 0, c))
    cot_spec = pl.BlockSpec((1, length, LANES), lambda c, k: (k, 0, c))
    turned_spec = pl.BlockSpec((per_chunk, 1, GROUP, length), turned_block)

    short_sums, u, e, states = pl.pallas_call(
        front_kernel,
        grid=(chunks, seqs),
        in_specs=[stream_spec, prev_spec, tap_spec, cot_spec, pl.BlockSpec((LANES, 1), lambda c, k: (c, 0))],
        out_specs=[stream_spec, turned_spec, turned_spec, pl.BlockSpec((1, 6 * POLES, LANES), lambda c, k: (c, 0, 0))],
        out_shape=[
            shape(streams.shape, f32),
            shape((groups, seqs, GROUP, length), bf16),
            shape((groups, seqs, GROUP, length), bf16),
            shape((chunks, 6 * POLES, LANES), f32),
        ],
        scratch_shapes=[pltpu.VMEM((3, length + HALO, LANES), f32), pltpu.VMEM((2, 2, LANES, length), bf16)],
        compiler_params=params(),
        name="front",
    )(streams, prev, taps, cotangent, rate_rows.reshape(groups * POLES, 1))

    slice_rows = chunks * 6 * POLES // count
    slots = (count, slice_rows, LANES)
    vmem = pl.BlockSpec(memory_space=pltpu.VMEM)
    anywhere = pl.BlockSpec(memory_space=pl.ANY)
    halo_shape = shape((groups, seqs, GROUP, LANES), bf16)
    carry, u_halo, e_halo = pl.pallas_call(
        functools.partial(exchange_kernel, count),
        in_specs=[vmem, vmem, anywhere, anywhere],
        out_specs=[vmem, anywhere, anywhere],
        out_shape=[shape(slots, f32), halo_shape, halo_shape],
        scratch_shapes=[
            pltpu.VMEM(slots, f32),
            pltpu.VMEM(slots, f32),
            pltpu.VMEM(slots, f32),
            pltpu.SemaphoreType.DMA((4, count)),
            pltpu.SemaphoreType.DMA((4,)),
        ],
        compiler_params=pltpu.CompilerParams(collective_id=0, has_side_effects=True),
        name="exchange",
    )(states.reshape(slots), decay.reshape(slots), u, e)

    own_spec = pl.BlockSpec((per_chunk, seqs, GROUP, length), lambda c: (c, 0, 0, 0))
    halo_spec = pl.BlockSpec((per_chunk, seqs, GROUP, LANES), lambda c: (c, 0, 0, 0))
    table_spec = lambda *tail: pl.BlockSpec((per_chunk,) + tail, lambda c: (c, 0, 0))
    smem = pl.BlockSpec(memory_space=pltpu.SMEM)
    s, w, lags = pl.pallas_call(
        long_kernel,
        grid=(chunks,),
        in_specs=[
            smem, own_spec, halo_spec, own_spec, halo_spec,
            pl.BlockSpec((1, 6 * POLES, LANES), lambda c: (c, 0, 0)),
            table_spec(POLES, 1), table_spec(POLES, 1), table_spec(1, MEDIUM), table_spec(1, 4 * MEDIUM),
        ],
        out_specs=[own_spec, own_spec, table_spec(1, LANES)],
        out_shape=[
            shape((groups, seqs, GROUP, length), f32),
            shape((groups, seqs, GROUP, length), f32),
            shape((groups, 1, LANES), f32),
        ],
        scratch_shapes=[pltpu.VMEM((LANES, 6 * POLES), f32)],
        compiler_params=params(),
        name="long",
    )(edges, u, u_halo, e, e_halo, carry.reshape(chunks, 6 * POLES, LANES), rate_cols, residue_cols, tap_rows, back_taps)

    filtered, grads, heads, tails, corr = pl.pallas_call(
        back_kernel,
        grid=(chunks, seqs),
        in_specs=[stream_spec, stream_spec, prev_spec, tap_spec, cot_spec, turned_spec, turned_spec],
        out_specs=[cot_spec, stream_spec, prev_spec, prev_spec, pl.BlockSpec((24, LANES), lambda c, k: (0, 0))],
        out_shape=[
            shape(cotangent.shape, bf16),
            shape(streams.shape, bf16),
            shape((3, seqs, HALO, width), f32),
            shape((3, seqs, HALO, width), f32),
            shape((24, LANES), f32),
        ],
        scratch_shapes=[
            pltpu.VMEM((3, length + HALO, LANES), f32),
            pltpu.VMEM((3, length + HALO, LANES), f32),
            pltpu.VMEM((length, LANES), f32),
            pltpu.VMEM((length, LANES), f32),
            pltpu.VMEM((3, 8, 8, LANES), f32),
        ],
        compiler_params=params(),
        name="back",
    )(short_sums, streams, prev, taps, cotangent, s, w)

    rows = 24 + groups
    corr_sum, lag_sum, next_heads = pl.pallas_call(
        functools.partial(reduce_kernel, count, across),
        in_specs=[vmem, vmem, anywhere],
        out_specs=[vmem, vmem, anywhere],
        out_shape=[shape((24, LANES), f32), shape((groups, LANES), f32), shape(heads.shape, f32)],
        scratch_shapes=[
            pltpu.VMEM((rows, LANES), f32),
            pltpu.VMEM((count, rows, LANES), f32),
            pltpu.VMEM((8, LANES), f32),
            pltpu.VMEM((across, 8, LANES), f32),
            pltpu.SemaphoreType.DMA((2, count)),
            pltpu.SemaphoreType.DMA((2, across)),
            pltpu.SemaphoreType.DMA((2,)),
        ],
        compiler_params=pltpu.CompilerParams(collective_id=1, has_side_effects=True),
        name="reduce",
    )(corr, lags.reshape(groups, LANES), heads)

    last = length // (2 * HALO) - 1
    whole = lambda *dims: pl.BlockSpec(dims, lambda i: (0,) * len(dims))
    last_spec = pl.BlockSpec((3, seqs, 2 * HALO, width), lambda i: (0, 0, last, 0))
    grads = pl.pallas_call(
        edge_kernel,
        grid=(1,),
        in_specs=[smem, last_spec, whole(3, seqs, HALO, width), whole(3, seqs, HALO, width), whole(3, 8, width)],
        out_specs=last_spec,
        out_shape=shape(grads.shape, bf16),
        input_output_aliases={1: 0},
        compiler_params=params(),
        name="edge",
    )(edges, grads, tails, next_heads, taps)
    short_grad = corr_sum.reshape(3, 8, LANES)[:, :SHORT, :groups]
    medium_grad = jnp.flip(lag_sum.T, 0)
    return filtered, grads, short_grad, medium_grad


def solution(mesh):
    in_specs = (
        P(None, None, "ctx", "ch"),
        P(None, None, "ch"),
        P(None, "ch"),
        P(None, "ch"),
        P(None, "ch"),
        P(None, "ctx", "ch"),
    )
    out_specs = (
        P(None, "ctx", "ch"),
        P(None, None, "ctx", "ch"),
        P(None, None, "ch"),
        P(None, "ch"),
    )
    return jax.shard_map(on_device, mesh=mesh, in_specs=in_specs, out_specs=out_specs, check_vma=False)
```

time: 556 us -> 153 us (0.28); the launches traced: 545 us -> 151 us
  local copies, waits for them, and re-layouts: 149 us -> 11.7 us
  Pallas kernels: 0 us -> 132 us
  other arithmetic: 120 us -> 2.66 us
  matrix products: 117 us -> 0 us
  blocking collectives: 116 us -> 0 us
  starting transfers between devices: 24.8 us -> 4.35 us
  between operations: 17.8 us -> 0.71 us
    pallas_call x0 -> x6, Pallas kernels: none -> 132 us  [the longest x1 52.7 us: on_device(): pl.pallas_call(long_kernel, grid=(chunks,), in_specs=[smem, own_spec, hal...]
    dot_general x11 -> x0, matrix products: 117 us -> none  [the longest x1 35 us: on_device(): jnp.einsum('gts,kbsgc->kbtgc', toeplitz, mixed_blocks, precision=highest)]
    psum x2 -> x0, blocking collectives: 94.6 us -> none  [the longest x1 67.3 us: on_device(): short_sum, medium_sum = lax.psum((short_local, medium_local), 'ctx')]
    reduce_sum x27 -> x0, other arithmetic: 48.1 us -> none  [the longest x3 36.6 us: on_device(): jnp.sum(grads[stream] * shifted.astype(jnp.float32), axis=(0, 1))]
    unnamed x210 -> x5, local copies, waits for them, and re-layouts: 38.7 us -> 1.25 us
    reshape x26 -> x2, local copies, waits for them, and re-layouts: 37.8 us -> 1.05 us  [the longest x1 0.86 us: on_device(): rate_rows.reshape(groups * POLES, 1)]
    another operation x6 -> x1, other arithmetic: 32.6 us -> 0.65 us  [on_device(): edges = jnp.stack([place, count - 1 - place]).astype(jnp.int32)]
    all_gather x1 -> x0, blocking collectives: 21.7 us -> none  [entering(): gathered = jax.tree.map(lambda a: lax.all_gather(a, axis), part)]
  transfers between devices with their start and end apart: 6 -> 1, of which waited for: 0 -> 0; matrix products, arithmetic and copies ran while one was open for 46% -> 7% of each run, Pallas kernels for 0% -> 0%
where the time goes in v1:
time: 153 us; the launch traced here: 151 us
  Pallas kernels  132 us (86%)
  local copies, waits for them, and re-layouts  11.7 us (8%)
  starting transfers between devices  4.35 us (3%)
  other arithmetic  2.66 us (2%)
    pallas_call x1, Pallas kernels, on_device(): pl.pallas_call(long_kernel, grid=(chunks,), in_specs=[smem, own_spec, hal...  52.7 us
    pallas_call x1, Pallas kernels, on_device(): pl.pallas_call(functools.partial(exchange_kernel, count), in_specs=[vmem,...  22.8 us
    pallas_call x1, Pallas kernels, on_device(): pl.pallas_call(functools.partial(reduce_kernel, count, across), in_specs=...  20.3 us
    pallas_call x1, Pallas kernels, on_device(): pl.pallas_call(back_kernel, grid=(chunks, seqs), in_specs=[stream_spec, s...  18.9 us
    pallas_call x1, Pallas kernels, on_device(): pl.pallas_call(front_kernel, grid=(chunks, seqs), in_specs=[stream_spec,...  15.1 us
    ppermute x1, starting transfers between devices, on_device(): lax.ppermute(streams[:, :, length - HALO:], 'ctx', [(i - 1, i) for i in r...  4.35 us
  transfers between devices with their start and end apart: 1, of which 0 were waited for; matrix products, arithmetic and copies ran while one was open for 7% of the time, Pallas kernels for 0%

profile of v1, /device:TPU:1, one launch (start us, length us, event | category | flops | bytes accessed | tf_op | source)
XLA Modules:
  0.0 151.1 jit_solution(10123806771322651186)
XLA Ops:
  0.6 0.9 slice.6
  1.5 4.4 %collective-permute-start = (bf16[3,3,8,512]{3,2,1,0:T(8,128)(2,1)S(1)}, bf16[3,3,8,512]{3,2,1,0:T(8,128)(2,1)S(1)}, u32[]{:S(2)}, u32[]{:S(2)}) collective-permute-start(bf16[3,3,8,512]{3,2,1,0:T(8,128)(2,1)S(1)} %slice.6), channel_id=1, source_target_pairs={{0,8},{8,16},{16,24},{24,32},{32,40},{40,48},{48,56},{56,64},{64,7... | collective-permute-start | bytes 221192 | tf_op jit(solution)/shard_map/ppermute | solution.py:448
  5.9 0.7 multiply_exponential_fusion
  6.6 0.8 copy.15
  7.4 1.3 convert_bitcast_fusion
  8.7 0.1 rev.8
  8.7 0.1 pad.9
  8.8 0.7 broadcast_in_dim.23.back_tap_ref
  9.5 0.9 reshape.36.rate_ref
  10.3 0.1 broadcast_in_dim.19
  10.5 0.1 reshape_reshape.3
  10.6 1.6 %copy.19.residue_ref = f32[32,16,1]{2,1,0:T(8,128)} copy(f32[32,16,1]{0,1,2:T(8,128)} %bitcast.34) | data formatting | bytes 4096 | tf_op jit(solution)/shard_map/broadcast_in_dim | solution.py:452
  12.2 1.6 %copy.18.rate_ref = f32[32,16,1]{2,1,0:T(8,128)} copy(f32[32,16,1]{0,1,2:T(8,128)} %bitcast.29) | data formatting | bytes 4096 | tf_op jit(solution)/shard_map/broadcast_in_dim | solution.py:451
  13.8 0.8 broadcast_in_dim.18
  14.6 0.2 reshape.30
  14.8 0.6 pad.8.tap_ref
  15.5 0.6 pad_add_fusion.edge_ref
  16.1 0.0 collective-permute-done.prev_ref
  16.1 0.0 copy-start
  16.1 0.6 copy-done
  16.7 15.1 %front.1 = (f32[3,3,512,512]{3,2,1,0:T(8,128)}, bf16[32,3,16,512]{3,2,1,0:T(8,128)(2,1)}, bf16[32,3,16,512]{3,2,1,0:T(8,128)(2,1)}, f32[4,96,128]{2,1,0:T(8,128)}) custom-call(bf16[3,3,512,512]{3,2,1,0:T(8,128)(2,1)} %stream_ref.3, bf16[3,3,8,512]{3,2,1,0:T(8,128)(2,1)} %copy-done, f32[3,8,512]{2,1,0:T(8,128)} %pad.8.tap_ref, bf16[3,512,512]{2,1,0:T(8,128)(2,1)} %cot_ref.3, ...), custom_call_target="tpu_custom_call" | custom-call | tf_op jit(solution)/shard_map/front/pallas_call | solution.py:468
  31.8 0.7 tile.8
  32.5 22.8 %exchange.1 = (f32[16,24,128]{2,1,0:T(8,128)}, bf16[32,3,16,128]{3,2,1,0:T(8,128)(2,1)}, bf16[32,3,16,128]{3,2,1,0:T(8,128)(2,1)}) custom-call(f32[16,24,128]{2,1,0:T(8,128)} %bitcast.26, f32[16,24,128]{2,1,0:T(8,128)} %bitcast.24, bf16[32,3,16,512]{3,2,1,0:T(8,128)(2,1)} %get-tuple-element.23.u_ref, bf16[32,3,16,512]{3,2,1,0:T(8,128)(2,1)} %get-tuple-element.25.e_ref), custom_call_target="tpu_custom_call" | custom-call | tf_op jit(solution)/shard_map/exchange/pallas_call | solution.py:489
  55.3 52.7 %long.1 = (f32[32,3,16,512]{3,2,1,0:T(8,128)}, f32[32,3,16,512]{3,2,1,0:T(8,128)}, f32[32,1,128]{2,1,0:T(1,128)}) custom-call(s32[2]{0:T(128)} %pad_add_fusion.edge_ref, bf16[32,3,16,512]{3,2,1,0:T(8,128)(2,1)} %get-tuple-element.23.u_ref, bf16[32,3,16,128]{3,2,1,0:T(8,128)(2,1)} %get-tuple-element.26.u_halo_ref, ...), custom_call_target="tpu_custom_call" | custom-call | tf_op jit(solution)/shard_map/long/pallas_call | solution.py:509
  108.0 18.9 %back.1 = (bf16[3,512,512]{2,1,0:T(8,128)(2,1)}, bf16[3,3,512,512]{3,2,1,0:T(8,128)(2,1)}, f32[3,3,8,512]{3,2,1,0:T(8,128)}, f32[3,3,8,512]{3,2,1,0:T(8,128)}, f32[24,128]{1,0:T(8,128)}) custom-call(f32[3,3,512,512]{3,2,1,0:T(8,128)} %get-tuple-element.22.short_ref, bf16[3,3,512,512]{3,2,1,0:T(8,128)(2,1)} %stream_ref.3, bf16[3,3,8,512]{3,2,1,0:T(8,128)(2,1)} %copy-done, ...), custom_call_target="tpu_custom_call" | custom-call | tf_op jit(solution)/shard_map/back/pallas_call | solution.py:528
  126.9 20.3 %reduce.1 = (f32[24,128]{1,0:T(8,128)}, f32[32,128]{1,0:T(8,128)}, f32[3,3,8,512]{3,2,1,0:T(8,128)}) custom-call(f32[24,128]{1,0:T(8,128)} %get-tuple-element.34.corr_ref, f32[32,128]{1,0:T(8,128)} %bitcast.32, f32[3,3,8,512]{3,2,1,0:T(8,128)} %get-tuple-element.36.head_ref), custom_call_target="tpu_custom_call" | custom-call | tf_op jit(solution)/shard_map/reduce/pallas_call | solution.py:552
  147.2 1.4 rev.9
  148.6 0.0 copy-start.1
  148.6 1.9 %edge.1 = bf16[3,3,512,512]{3,2,1,0:T(8,128)(2,1)} custom-call(s32[2]{0:T(128)} %pad_add_fusion.edge_ref, bf16[3,3,512,512]{3,2,1,0:T(8,128)(2,1)} %get-tuple-element.32.grad_ref, f32[3,3,8,512]{3,2,1,0:T(8,128)} %get-tuple-element.33.tail_ref, f32[3,3,8,512]{3,2,1,0:T(8,128)} %get-tuple-element.37.head_ref, ...), custom_call_target="tpu_custom_call", output_to_operand_aliasing={{}: (1, {})} | custom-call | tf_op jit(solution)/shard_map/edge/pallas_call | solution.py:573
  150.5 0.0 copy-done.1
  150.5 0.6 copy.23
  (1 shorter events, 0.0 us)
Async XLA Ops:
  1.5 14.6 %collective-permute-start = (bf16[3,3,8,512]{3,2,1,0:T(8,128)(2,1)S(1)}, bf16[3,3,8,512]{3,2,1,0:T(8,128)(2,1)S(1)}, u32[]{:S(2)}, u32[]{:S(2)}) collective-permute-start(bf16[3,3,8,512]{3,2,1,0:T(8,128)(2,1)S(1)} %slice.6), channel_id=1, source_target_pairs={{0,8},{8,16},{16,24},{24,32},{32,40},{40,48},{48,56},{56,64},{64,7... | collective-permute-start | bytes 221192 | tf_op jit(solution)/shard_map/ppermute | solution.py:448
  16.1 0.6 copy-start
  148.6 1.9 %copy-start.1 = (f32[24,128]{1,0:T(8,128)S(1)}, f32[24,128]{1,0:T(8,128)}, u32[]{:S(2)}) copy-start(f32[24,128]{1,0:T(8,128)} %get-tuple-element.38) | copy-start | bytes 36868

commit v2 on v1

v2 whole, which is shorter than its diff:
```python
import functools

import jax
import jax.numpy as jnp
from jax import lax
from jax.experimental import pallas as pl
from jax.experimental.pallas import tpu as pltpu
from jax.sharding import PartitionSpec as P

GROUP = 16
SHORT = 7
MEDIUM = 128
POLES = 16
LANES = 128
HALO = 8
MESH = pl.DeviceIdType.MESH
VMEM_LIMIT = 58 * 1024 * 1024

clip_norm = 100.0
highest = lax.Precision.HIGHEST
f32 = jnp.float32
bf16 = jnp.bfloat16
NN = (((1,), (0,)), ((), ()))
NT = (((1,), (1,)), ((), ()))


def matmul(a, b, dims=NN, precision=None):
    return lax.dot_general(a, b, dims, precision=precision, preferred_element_type=f32)


def group_mask(shape, row_unit, lane_unit):
    rows = lax.broadcasted_iota(jnp.int32, shape, 0) // row_unit
    lanes = lax.broadcasted_iota(jnp.int32, shape, 1) // lane_unit
    return rows == lanes


def fill_rows(rows_ref, stream_ref, prev, index):
    rows_ref[index, :HALO] = prev
    rows_ref[index, HALO:] = stream_ref[index, 0].astype(f32)


def spread(table, chunk):
    rows = lax.broadcasted_iota(jnp.int32, (table.shape[1], LANES), 0)
    lanes = lax.broadcasted_iota(jnp.int32, (table.shape[1], LANES), 1) // GROUP + chunk * (LANES // GROUP)
    return matmul(table, jnp.where(rows == lanes, 1.0, 0.0), precision=highest)


def remote(source, target, send_sem, recv_sem, axis, peer):
    return pltpu.make_async_remote_copy(
        src_ref=source, dst_ref=target, send_sem=send_sem, recv_sem=recv_sem, device_id={axis: peer}, device_id_type=MESH
    )


def front_kernel(count, stream_ref, whole_ref, short_filter_ref, cot_ref, rate_ref,
                 short_ref, u_ref, e_ref, prev_ref, tap_ref, carry_ref, u_halo_ref, e_halo_ref,
                 rows_ref, weight_ref, filter_ref, prev_got, u_edge, e_edge, states, got, scan, back,
                 row_sems, halo_sems, sems):
    chunk = pl.program_id(0)
    seq = pl.program_id(1)
    chunks = pl.num_programs(0)
    seqs = pl.num_programs(1)
    length = stream_ref.shape[2]
    block = 64
    quarter = count // 4
    me = lax.axis_index("ctx")
    after = lax.rem(me + 1, count)
    before = lax.rem(me + count - 1, count)
    first_step = (chunk == 0) & (seq == 0)
    last_step = (chunk == chunks - 1) & (seq == seqs - 1)
    barrier = pltpu.get_barrier_semaphore()
    stream_copy = remote(whole_ref.at[:, :, pl.ds(length - HALO, HALO), :], prev_got, row_sems.at[0], row_sems.at[1], "ctx", after)

    @pl.when(first_step)
    def _():
        for step in range(1, count):
            pl.semaphore_signal(barrier, inc=1, device_id={"ctx": lax.rem(me + step, count)}, device_id_type=MESH)

    @pl.when(seq == 0)
    def _():
        filter_ref[...] = jnp.zeros_like(filter_ref)
        for stream in range(3):
            filter_ref[8 * stream : 8 * stream + SHORT] = short_filter_ref[stream]
        tap_ref[...] = spread(filter_ref[...], chunk).reshape(3, 8, LANES)
        tiled = jnp.concatenate([rate_ref[...]] * (LANES // POLES), axis=0)
        row = lax.broadcasted_iota(jnp.int32, tiled.shape, 0) // POLES + chunk * (LANES // POLES)
        lane = lax.broadcasted_iota(jnp.int32, tiled.shape, 1)
        rate = jnp.sum(jnp.where(row == lane, tiled, 0.0), axis=1, keepdims=True)
        step = lax.broadcasted_iota(jnp.int32, (LANES, length), 1).astype(f32)
        for way in range(2):
            ago = (length - 1.0) - step if way == 0 else step
            full = jnp.exp(-rate * ago)
            high = full.astype(bf16)
            weight_ref[way, 0] = high
            weight_ref[way, 1] = (full - high.astype(f32)).astype(bf16)

    @pl.when(first_step)
    def _():
        pl.semaphore_wait(barrier, count - 1)
        stream_copy.start()

    for stream in range(3):
        rows_ref[stream, HALO:] = stream_ref[stream, 0].astype(f32)
    u_parts = []
    e_parts = []
    for first in reversed(range(0, length, block)):
        if first == 0:
            @pl.when(first_step)
            def _():
                stream_copy.wait()
                for stream in range(3):
                    for one in range(3):
                        rows = prev_got[stream, one].astype(f32)
                        prev_ref[stream, one] = jnp.where(me > 0, rows, 0.0)

            for stream in range(3):
                rows_ref[stream, :HALO] = prev_ref[stream, seq, :, pl.ds(pl.multiple_of(chunk * LANES, LANES), LANES)]
        sums = []
        for stream in range(3):
            total = None
            for offset in range(SHORT):
                begin = first + HALO - offset
                term = tap_ref[stream, offset : offset + 1, :] * rows_ref[stream, begin : begin + block, :]
                total = term if total is None else total + term
            short_ref[stream, 0, first : first + block, :] = total
            sums.append(total)
        u_parts.insert(0, (sums[1] * sums[2]).astype(bf16))
        e_parts.insert(0, (cot_ref[0, first : first + block, :].astype(f32) * sums[0]).astype(bf16))
    u = jnp.concatenate(u_parts, axis=0)
    e = jnp.concatenate(e_parts, axis=0)
    turned = u.T.reshape(LANES // GROUP, GROUP, length)
    u_ref[:, 0] = turned
    u_edge[chunk, :, seq] = turned[:, :, length - LANES :]
    turned = e.T.reshape(LANES // GROUP, GROUP, length)
    e_ref[:, 0] = turned
    e_edge[chunk, :, seq] = turned[:, :, :LANES]
    mask = group_mask((LANES, LANES), POLES, GROUP)
    for way, value in ((0, u), (1, e)):
        every = matmul(weight_ref[way, 0], value) + matmul(weight_ref[way, 1], value)
        own = jnp.where(mask, every, 0.0).reshape(LANES // POLES, POLES, LANES).sum(axis=0)
        row = pl.multiple_of(8 * seq, 8)
        states[4 * chunk + 2 * way, pl.ds(row, 8), :] = own[:8]
        states[4 * chunk + 2 * way + 1, pl.ds(row, 8), :] = own[8:]

    def halo_copies(c):
        groups = pl.ds(pl.multiple_of(c * (LANES // GROUP), LANES // GROUP), LANES // GROUP)
        return (
            remote(u_edge.at[c], u_halo_ref.at[groups], halo_sems.at[0, c], halo_sems.at[1, c], "ctx", after),
            remote(e_edge.at[c], e_halo_ref.at[groups], halo_sems.at[2, c], halo_sems.at[3, c], "ctx", before),
        )

    @pl.when(seq == seqs - 1)
    def _():
        for part in range(4):
            peer = quarter * chunk + part

            @pl.when(peer != me)
            def _():
                remote(states.at[peer], got.at[me], sems.at[0, peer], sems.at[1, me], "ctx", peer).start()

        for copy in halo_copies(chunk):
            copy.start()

    @pl.when(last_step)
    def _():
        got[pl.ds(me, 1)] = states[pl.ds(me, 1)]
        decay = jnp.exp(-float(length) * spread(rate_ref[...], me // quarter))
        decay = jnp.where(lax.rem(me, 2) == 0, decay[:8], decay[8:])
        decay = jnp.concatenate([decay] * 3, axis=0)
        forward = lax.rem(me, 4) < 2
        for step in range(1, count):
            peer = lax.rem(me + step, count)
            remote(states.at[peer], got.at[peer], sems.at[0, peer], sems.at[1, peer], "ctx", peer).wait_recv()
        running = jnp.zeros_like(decay)
        ahead = []
        for source in range(count):
            ahead.append(running)
            running = decay * running + got[source]
        running = jnp.zeros_like(decay)
        behind = [None] * count
        for source in reversed(range(count)):
            behind[source] = running
            running = decay * running + got[source]
        for target in range(count):
            scan[target] = jnp.where(forward, ahead[target], behind[target])
        for step in range(1, count):
            peer = lax.rem(me + step, count)
            remote(scan.at[peer], back.at[me], sems.at[2, peer], sems.at[3, me], "ctx", peer).start()
        back[pl.ds(me, 1)] = scan[pl.ds(me, 1)]
        for step in range(1, count):
            peer = lax.rem(me + step, count)
            remote(scan.at[peer], back.at[peer], sems.at[2, peer], sems.at[3, peer], "ctx", peer).wait_recv()
        carry_ref[...] = back[...]
        for step in range(1, count):
            peer = lax.rem(me + step, count)
            remote(states.at[peer], got.at[me], sems.at[0, peer], sems.at[1, me], "ctx", peer).wait_send()
            remote(scan.at[peer], back.at[me], sems.at[2, peer], sems.at[3, me], "ctx", peer).wait_send()
        for c in range(4):
            for copy in halo_copies(c):
                copy.wait()


def slanted(row, first_zero=False):
    lane = lax.broadcasted_iota(jnp.int32, (LANES, LANES), 1)
    here = lane >= lax.broadcasted_iota(jnp.int32, (LANES, LANES), 0)
    tiles = []
    earlier = jnp.zeros((LANES, LANES), f32)
    for j in range(row.shape[1] // LANES):
        part = jnp.broadcast_to(row[:, LANES * j : LANES * (j + 1)], (LANES, LANES))
        moved = pltpu.roll(part, 0, 1, stride=1, stride_axis=0)
        tiles.append(jnp.where(here, moved, earlier).astype(bf16))
        earlier = moved
    return tiles, jnp.where(here, 0.0, earlier).astype(bf16)


def split(value):
    high = value.astype(bf16)
    return high, (value - high.astype(f32)).astype(bf16)


def long_kernel(u_ref, u_halo_ref, e_ref, e_halo_ref, carry_ref, rate_ref, residue_ref, tap_ref, s_ref, w_ref, lag_ref, turned_ref):
    chunk = pl.program_id(0)
    place = lax.axis_index("ctx")
    count = lax.axis_size("ctx")
    length = u_ref.shape[3]
    half = length // 2
    per_step = u_ref.shape[0]
    rows = 3 * GROUP
    has_prev = place > 0
    has_next = place < count - 1
    parts = []
    for way in range(2):
        for seq in range(3):
            parts += [carry_ref[2 * way, 8 * seq : 8 * seq + 8], carry_ref[2 * way + 1, 8 * seq : 8 * seq + 8]]
    turned_ref[...] = jnp.concatenate(parts, axis=0).T
    zero = jnp.zeros((LANES, LANES), bf16)
    eye = group_mask((POLES, POLES), 1, 1)

    def lanes(shape):
        return lax.broadcasted_iota(jnp.int32, shape, 1).astype(f32)

    def one(index):
        group = chunk * per_step + index
        pick = lax.broadcasted_iota(jnp.int32, rate_ref.shape, 1) == group
        rate = jnp.sum(jnp.where(pick, rate_ref[...], 0.0), axis=1, keepdims=True)
        residue = jnp.sum(jnp.where(pick, residue_ref[...], 0.0), axis=1, keepdims=True)
        rate_row = jnp.sum(jnp.where(eye, rate, 0.0), axis=0, keepdims=True)
        carry = turned_ref[pl.ds(pl.multiple_of(index * GROUP, GROUP), GROUP), :]
        ahead = jnp.concatenate([carry[:, POLES * j : POLES * (j + 1)] for j in range(3)], axis=0)
        behind = jnp.concatenate([carry[:, POLES * j : POLES * (j + 1)] for j in range(3, 6)], axis=0)
        u_halo = jnp.where(has_prev, u_halo_ref[index].reshape(rows, LANES), jnp.zeros((), bf16))
        e_halo = jnp.where(has_next, e_halo_ref[index].reshape(rows, LANES), jnp.zeros((), bf16))
        u_own = u_ref[index].reshape(rows, length)
        e_own = e_ref[index].reshape(rows, length)
        u_ext = jnp.concatenate([u_halo, u_own], axis=1)
        edge = lanes((POLES, LANES))

        def local_state(value, ago):
            high, low = split(jnp.exp(-rate * ago))
            return matmul(jnp.concatenate([value, value], axis=1), jnp.concatenate([high, low], axis=1), NT)

        def columns(parts):
            values = [split(part) for part in parts]
            high = jnp.concatenate([value[0] for value in values], axis=0)
            low = jnp.concatenate([value[1] for value in values], axis=0)
            return jnp.concatenate([high, low, high], axis=1)

        def weights(value):
            high, low = split(value)
            return jnp.concatenate([high, high, low], axis=0)

        near = jnp.exp(-float(half) * rate_row)
        ahead = ahead - local_state(u_halo, (LANES - 1.0) - edge)
        ahead_columns = columns([ahead, ahead * near])
        far = (behind - local_state(e_halo, edge)) * jnp.exp(float(half) * rate_row)
        behind_columns = columns([behind * near, behind, far])

        lag = lanes((POLES, 5 * LANES))
        h_row = jnp.sum(residue * jnp.exp(-rate * lag), axis=0, keepdims=True)
        h_tiles, _ = slanted(h_row)
        taps = tap_ref[pl.ds(group, 1), :].astype(f32)
        q = matmul(jnp.broadcast_to(taps, (16, LANES)).astype(bf16), jnp.concatenate(h_tiles, axis=1))[:1]
        q_tiles, _ = slanted(q)
        k_tiles, k_last = slanted(taps)
        k_tile = k_tiles[0]

        moment = jnp.sum(taps * jnp.exp(rate * edge), axis=1, keepdims=True)
        time = lanes((POLES, half))
        ahead_weights = weights(residue * moment * jnp.exp(-rate * (time + 1.0)))
        behind_weights = weights(residue * jnp.exp(-rate * (half - time)))

        left = jnp.concatenate([jnp.concatenate([jnp.zeros((rows, half), bf16), u_ext[:, : 3 * LANES]], axis=1), u_ext], axis=0)
        left_tiles = [zero] + q_tiles
        right = jnp.concatenate(
            [jnp.concatenate([left_tiles[4 - b], left_tiles[5 - b]], axis=1) for b in range(5)], axis=0
        )
        s = matmul(left, right) + matmul(ahead_columns, ahead_weights)
        s_ref[index] = jnp.concatenate([s[:rows], s[rows:]], axis=1).reshape(3, GROUP, length)

        left = jnp.concatenate(
            [
                e_own,
                jnp.concatenate([e_own[:, half:], jnp.zeros((rows, half), bf16)], axis=1),
                jnp.concatenate([e_halo, jnp.zeros((rows, length - LANES), bf16)], axis=1),
            ],
            axis=0,
        )
        right = jnp.concatenate(
            [jnp.concatenate(h_tiles[:4], axis=1), jnp.concatenate([zero] + h_tiles[:3], axis=1)], axis=0
        )
        p = matmul(left, right, NT) + matmul(behind_columns, behind_weights)
        tail = jnp.where(has_next, p[2 * rows :, :LANES], 0.0)
        p = jnp.concatenate([p[:rows], p[rows : 2 * rows], tail], axis=1).astype(bf16)

        left = jnp.concatenate([p[:, : 3 * LANES], p[:, half:]], axis=0)
        right = jnp.concatenate(
            [jnp.concatenate([k_tile, k_last, zero], axis=1), jnp.concatenate([zero, k_tile, k_last], axis=1)], axis=0
        )
        w = matmul(left, right, NT)
        w_ref[index] = jnp.concatenate([w[:rows], w[rows:]], axis=1).reshape(3, GROUP, length)

        p_stack = jnp.concatenate([p[:, LANES * b : LANES * (b + 1)] for b in range(4)], axis=0)
        u_stack = jnp.concatenate([u_ext[:, LANES * b : LANES * (b + 2)] for b in range(4)], axis=0)
        table = matmul(p_stack.T, u_stack)
        total = table[LANES - 8 :]
        for tile in reversed(range(LANES // 8 - 1)):
            total = pltpu.roll(total, 2 * LANES - 8, 1) + table[8 * tile : 8 * tile + 8]
        sub = lax.broadcasted_iota(jnp.int32, total.shape, 0)
        for bit in (1, 2, 4):
            total = jnp.where((sub & bit) > 0, pltpu.roll(total, 2 * LANES - bit, 1), total)
        total = jnp.sum(total, axis=0, keepdims=True)
        lag_ref[index] = pltpu.roll(total, 2 * LANES - 1, 1)[:, :LANES]

    def body(step, carry):
        one(2 * step)
        one(2 * step + 1)
        return carry

    lax.fori_loop(0, per_step // 2, body, 0)


def back_kernel(short_ref, stream_ref, prev_ref, tap_ref, cot_ref, s_ref, w_ref, out_ref, grad_ref, head_ref, tail_ref, corr_ref,
                rows_ref, g_ref, s_rows, w_rows, acc_ref):
    chunk = pl.program_id(0)
    seq = pl.program_id(1)
    length = stream_ref.shape[2]
    block = 64

    @pl.when(seq == 0)
    def _():
        acc_ref[...] = jnp.zeros_like(acc_ref)

    for stream in range(3):
        fill_rows(rows_ref, stream_ref, prev_ref[stream, 0], stream)
        g_ref[stream, length:] = jnp.zeros((HALO, LANES), f32)
    s_rows[...] = s_ref[:, 0].reshape(LANES, length).T
    w_rows[...] = w_ref[:, 0].reshape(LANES, length).T
    for first in range(0, length, block):
        here = slice(first, first + block)
        s = s_rows[here]
        w = w_rows[here]
        cot = cot_ref[0, here].astype(f32)
        out_ref[0, here] = (short_ref[0, 0, here] * s).astype(bf16)
        g_ref[0, here] = cot * s
        g_ref[1, here] = w * short_ref[2, 0, here]
        g_ref[2, here] = w * short_ref[1, 0, here]
    for stream in range(3):
        head_ref[stream, 0] = g_ref[stream, :HALO].astype(bf16)
        for first in range(0, length, block):
            total = None
            own = g_ref[stream, first : first + block]
            for offset in range(SHORT):
                term = tap_ref[stream, offset : offset + 1, :] * g_ref[stream, first + offset : first + offset + block]
                total = term if total is None else total + term
                begin = first + HALO - offset
                part = (own * rows_ref[stream, begin : begin + block]).reshape(block // 8, 8, LANES).sum(axis=0)
                acc_ref[stream, offset] += part
            grad_ref[stream, 0, first : first + block] = total.astype(bf16)
            if first + block == length:
                tail_ref[stream, 0] = total[block - HALO :]

    @pl.when(seq == pl.num_programs(1) - 1)
    def _():
        lane = lax.broadcasted_iota(jnp.int32, (LANES, LANES), 0) // GROUP + chunk * (LANES // GROUP)
        pick = jnp.where(lane == lax.broadcasted_iota(jnp.int32, (LANES, LANES), 1), 1.0, 0.0)
        sums = acc_ref[...].sum(axis=2).reshape(3 * 8, LANES)
        value = matmul(sums, pick, precision=highest)

        @pl.when(chunk == 0)
        def _():
            corr_ref[...] = value

        @pl.when(chunk > 0)
        def _():
            corr_ref[...] += value


def reduce_kernel(count, across, corr_ref, lag_ref, head_ref, corr_out, lag_out, head_out, mine, row_got, row_sum, col_got, norm_mine, norm_got,
                  row_sems, col_sems, norm_sems, head_sems):
    inner = 4
    me = lax.axis_index("ctx")
    ch = lax.axis_index("ch")
    col = lax.rem(me, inner)
    row = me // inner
    before = lax.rem(me + count - 1, count)
    after = lax.rem(me + 1, count)
    outer = count // inner

    def in_row(step):
        place = lax.rem(col + step, inner)
        return place, row * inner + place

    def in_col(step):
        place = lax.rem(row + step, outer)
        return place, place * inner + col

    def in_ch(step):
        place = lax.rem(ch + step, across)
        return place, place

    barrier = pltpu.get_barrier_semaphore()
    peers = [in_row(step)[1] for step in range(1, inner)] + [in_col(step)[1] for step in range(1, outer)] + [before, after]
    for peer in peers:
        pl.semaphore_signal(barrier, inc=1, device_id={"ctx": peer}, device_id_type=MESH)
    for step in range(1, across):
        pl.semaphore_signal(barrier, inc=1, device_id={"ch": in_ch(step)[1]}, device_id_type=MESH)
    pl.semaphore_wait(barrier, len(peers) + across - 1)
    top = corr_ref.shape[0]
    mine[:top] = corr_ref[...]
    mine[top:] = lag_ref[...]

    def gather(source, target, sems, axis, size, here, peer_of, between=None):
        copies = []
        for step in range(1, size):
            place, peer = peer_of(step)
            copies.append(remote(source, target.at[here], sems.at[0, place], sems.at[1, here], axis, peer))
        for copy in copies:
            copy.start()
        if between is not None:
            between()
        target[pl.ds(here, 1)] = source[...][None]
        for step in range(1, size):
            place, peer = peer_of(step)
            remote(source, target.at[place], sems.at[0, place], sems.at[1, place], axis, peer).wait_recv()
        total = target[0]
        for place in range(1, size):
            total = total + target[place]
        return total, copies

    head = remote(head_ref, head_out, head_sems.at[0], head_sems.at[1], "ctx", before)
    total, sent = gather(mine, row_got, row_sems, "ctx", inner, col, in_row, head.start)
    row_sum[...] = total
    total, more = gather(row_sum, col_got, col_sems, "ctx", outer, row, in_col)
    sent = sent + more
    norm_mine[...] = jnp.sum((total * total).reshape(total.shape[0] // 8, 8, LANES), axis=0)
    squares, more = gather(norm_mine, norm_got, norm_sems, "ch", across, ch, in_ch)
    sent = sent + more
    norm = jnp.sqrt(jnp.sum(jnp.sum(squares, axis=1, keepdims=True), axis=0, keepdims=True))
    factor = jnp.minimum(1.0, clip_norm / (norm + 1e-06))
    corr_out[...] = (total[:top] * factor).reshape(3, 8, LANES)[:, :SHORT, : corr_out.shape[2]]
    turn = lax.broadcasted_iota(jnp.int32, (LANES, LANES), 0) + lax.broadcasted_iota(jnp.int32, (LANES, LANES), 1) == LANES - 1
    lag_out[...] = matmul(total[top:] * factor, jnp.where(turn, 1.0, 0.0), precision=highest)
    for copy in sent:
        copy.wait_send()
    head.wait()


def edge_kernel(grad_ref, tail_ref, head_ref, tap_ref, out_ref):
    has_next = lax.axis_index("ctx") < lax.axis_size("ctx") - 1
    for stream in range(3):
        for seq in range(3):
            head = jnp.where(has_next, head_ref[stream, seq].astype(f32), 0.0)
            wide = jnp.concatenate([jnp.zeros((HALO, head.shape[1]), f32), head], axis=0)
            total = tail_ref[stream, seq]
            for offset in range(1, SHORT):
                total = total + tap_ref[stream, offset : offset + 1, :] * wide[offset : offset + HALO]
            low = jnp.concatenate([jnp.zeros_like(total), total], axis=0).astype(bf16)
            keep = lax.broadcasted_iota(jnp.int32, low.shape, 0) < HALO
            out_ref[stream, seq] = jnp.where(keep, grad_ref[stream, seq], low)


def params(**more):
    return pltpu.CompilerParams(vmem_limit_bytes=VMEM_LIMIT, **more)


def on_device(streams, short_filter, medium_filter, rates, residues, cotangent):
    count = lax.axis_size("ctx")
    across = lax.axis_size("ch")
    seqs, length, width = streams.shape[1:]
    groups = width // GROUP
    chunks = width // LANES
    per_chunk = LANES // GROUP
    shape = jax.ShapeDtypeStruct
    vmem = pl.BlockSpec(memory_space=pltpu.VMEM)
    anywhere = pl.BlockSpec(memory_space=pl.ANY)
    whole = lambda *dims: pl.BlockSpec(dims, lambda *steps: (0,) * len(dims))

    chunk_block = lambda c, k: (0, k, 0, c)
    turned_block = lambda c, k: (c, k, 0, 0)
    stream_spec = pl.BlockSpec((3, 1, length, LANES), chunk_block)
    prev_spec = pl.BlockSpec((3, 1, HALO, LANES), chunk_block)
    tap_spec = pl.BlockSpec((3, 8, LANES), lambda c, k: (0, 0, c))
    cot_spec = pl.BlockSpec((1, length, LANES), lambda c, k: (k, 0, c))
    turned_spec = pl.BlockSpec((per_chunk, 1, GROUP, length), turned_block)
    edge_shape = (3, seqs, HALO, width)
    slots = (count, 3 * 8, LANES)
    halo_shape = shape((groups, seqs, GROUP, LANES), bf16)

    short_sums, u, e, prev, taps, carry, u_halo, e_halo = pl.pallas_call(
        functools.partial(front_kernel, count),
        grid=(chunks, seqs),
        in_specs=[stream_spec, anywhere, whole(*short_filter.shape), cot_spec, whole(*rates.shape)],
        out_specs=[
            stream_spec, turned_spec, turned_spec, whole(*edge_shape), tap_spec, whole(*slots), anywhere, anywhere,
        ],
        out_shape=[
            shape(streams.shape, f32),
            shape((groups, seqs, GROUP, length), bf16),
            shape((groups, seqs, GROUP, length), bf16),
            shape(edge_shape, f32),
            shape((3, 8, width), f32),
            shape(slots, f32),
            halo_shape,
            halo_shape,
        ],
        scratch_shapes=[
            pltpu.VMEM((3, length + HALO, LANES), f32),
            pltpu.VMEM((2, 2, LANES, length), bf16),
            pltpu.VMEM((24, groups), f32),
            pltpu.VMEM(edge_shape, bf16),
            pltpu.VMEM((chunks, per_chunk, seqs, GROUP, LANES), bf16),
            pltpu.VMEM((chunks, per_chunk, seqs, GROUP, LANES), bf16),
            pltpu.VMEM(slots, f32),
            pltpu.VMEM(slots, f32),
            pltpu.VMEM(slots, f32),
            pltpu.VMEM(slots, f32),
            pltpu.SemaphoreType.DMA((2,)),
            pltpu.SemaphoreType.DMA((4, chunks)),
            pltpu.SemaphoreType.DMA((4, count)),
        ],
        compiler_params=params(collective_id=0, has_side_effects=True),
        name="front",
    )(streams, streams, short_filter, cotangent, rates)

    own_spec = pl.BlockSpec((per_chunk, seqs, GROUP, length), lambda c: (c, 0, 0, 0))
    halo_spec = pl.BlockSpec((per_chunk, seqs, GROUP, LANES), lambda c: (c, 0, 0, 0))
    s, w, lags = pl.pallas_call(
        long_kernel,
        grid=(chunks,),
        in_specs=[
            own_spec, halo_spec, own_spec, halo_spec, pl.BlockSpec((4, 24, LANES), lambda c: (c, 0, 0)),
            whole(*rates.shape), whole(*rates.shape), whole(groups, MEDIUM),
        ],
        out_specs=[own_spec, own_spec, pl.BlockSpec((per_chunk, 1, LANES), lambda c: (c, 0, 0))],
        out_shape=[
            shape((groups, seqs, GROUP, length), f32),
            shape((groups, seqs, GROUP, length), f32),
            shape((groups, 1, LANES), f32),
        ],
        scratch_shapes=[pltpu.VMEM((LANES, 6 * POLES), f32)],
        compiler_params=params(),
        name="long",
    )(u, u_halo, e, e_halo, carry, rates, residues, medium_filter.astype(f32).T)

    filtered, grads, heads, tails, corr = pl.pallas_call(
        back_kernel,
        grid=(chunks, seqs),
        in_specs=[stream_spec, stream_spec, prev_spec, tap_spec, cot_spec, turned_spec, turned_spec],
        out_specs=[cot_spec, stream_spec, prev_spec, prev_spec, whole(24, LANES)],
        out_shape=[
            shape(cotangent.shape, bf16),
            shape(streams.shape, bf16),
            shape(edge_shape, bf16),
            shape(edge_shape, f32),
            shape((24, LANES), f32),
        ],
        scratch_shapes=[
            pltpu.VMEM((3, length + HALO, LANES), f32),
            pltpu.VMEM((3, length + HALO, LANES), f32),
            pltpu.VMEM((length, LANES), f32),
            pltpu.VMEM((length, LANES), f32),
            pltpu.VMEM((3, 8, 8, LANES), f32),
        ],
        compiler_params=params(),
        name="back",
    )(short_sums, streams, prev, taps, cotangent, s, w)

    sums = (24 + groups, LANES)
    short_grad, medium_grad, next_heads = pl.pallas_call(
        functools.partial(reduce_kernel, count, across),
        in_specs=[vmem, vmem, anywhere],
        out_specs=[vmem, vmem, anywhere],
        out_shape=[shape(short_filter.shape, f32), shape((groups, LANES), f32), shape(edge_shape, bf16)],
        scratch_shapes=[
            pltpu.VMEM(sums, f32),
            pltpu.VMEM((4,) + sums, f32),
            pltpu.VMEM(sums, f32),
            pltpu.VMEM((count // 4,) + sums, f32),
            pltpu.VMEM((8, LANES), f32),
            pltpu.VMEM((across, 8, LANES), f32),
            pltpu.SemaphoreType.DMA((2, 4)),
            pltpu.SemaphoreType.DMA((2, count // 4)),
            pltpu.SemaphoreType.DMA((2, across)),
            pltpu.SemaphoreType.DMA((2,)),
        ],
        compiler_params=pltpu.CompilerParams(collective_id=1, has_side_effects=True),
        name="reduce",
    )(corr, lags.reshape(groups, LANES), heads)

    last = length // (2 * HALO) - 1
    last_spec = pl.BlockSpec((3, seqs, 2 * HALO, width), lambda i: (0, 0, last, 0))
    grads = pl.pallas_call(
        edge_kernel,
        grid=(1,),
        in_specs=[last_spec, whole(*edge_shape), whole(*edge_shape), whole(3, 8, width)],
        out_specs=last_spec,
        out_shape=shape(grads.shape, bf16),
        input_output_aliases={0: 0},
        compiler_params=params(),
        name="edge",
    )(grads, tails, next_heads, taps)
    return filtered, grads, short_grad, medium_grad.T


def solution(mesh):
    in_specs = (
        P(None, None, "ctx", "ch"),
        P(None, None, "ch"),
        P(None, "ch"),
        P(None, "ch"),
        P(None, "ch"),
        P(None, "ctx", "ch"),
    )
    out_specs = (
        P(None, "ctx", "ch"),
        P(None, None, "ctx", "ch"),
        P(None, None, "ch"),
        P(None, "ch"),
    )
    return jax.shard_map(on_device, mesh=mesh, in_specs=in_specs, out_specs=out_specs, check_vma=False)
```

time: 153 us -> 125 us (0.82)
  Pallas kernels: 132 us -> 121 us
  local copies, waits for them, and re-layouts: 11.7 us -> 1.21 us
  starting transfers between devices: 4.35 us -> 0 us
    pallas_call x4 -> x3, Pallas kernels: 92.4 us -> 82.9 us  [the longest x1 45.8 us: on_device(): pl.pallas_call(long_kernel, grid=(chunks,), in_specs=[own_spec, halo_spec...]
    broadcast_in_dim x5 -> x0, local copies, waits for them, and re-layouts: 4.78 us -> none  [the longest x1 1.57 us: on_device(): rate_cols = rate_rows[:, :, None]]
    ppermute x1 -> x0, starting transfers between devices: 4.35 us -> none  [on_device(): lax.ppermute(streams[:, :, length - HALO:], 'ctx', [(i - 1, i) for i in r...]
  transfers between devices with their start and end apart: 1 -> 0, of which waited for: 0 -> 0; matrix products, arithmetic and copies ran while one was open for 7% -> 0% of each run, Pallas kernels for 0% -> 0%
where the time goes in v2:
time: 125 us; the launch traced here: 124 us
  Pallas kernels  121 us (97%)
  other arithmetic  1.3 us (1%)
    pallas_call x1, Pallas kernels, on_device(): pl.pallas_call(long_kernel, grid=(chunks,), in_specs=[own_spec, halo_spec...  45.8 us
    pallas_call x1, Pallas kernels, on_device(): pl.pallas_call(functools.partial(front_kernel, count), grid=(chunks, seqs...  35.2 us
    pallas_call x1, Pallas kernels, on_device(): pl.pallas_call(functools.partial(reduce_kernel, count, across), in_specs=...  19.5 us
    pallas_call x1, Pallas kernels, on_device(): pl.pallas_call(back_kernel, grid=(chunks, seqs), in_specs=[stream_spec, s...  18.9 us

profile of v2, /device:TPU:1, one launch (start us, length us, event | category | flops | bytes accessed | tf_op | source)
XLA Modules:
  0.0 124.4 jit_solution(14536513101730372544)
XLA Ops:
  0.6 1.3 %convert_bitcast_fusion.tap_ref = f32[32,128]{1,0:T(8,128)} fusion(bf16[128,32]{0,1:T(8,128)(2,1)} %param.8), kind=kLoop, calls=%fused_computation | loop fusion | flops 4096 | bytes 24576 | tf_op jit(solution)/shard_map/transpose | solution.py:562
  1.9 35.2 %front.1 = (f32[3,3,512,512]{3,2,1,0:T(8,128)}, bf16[32,3,16,512]{3,2,1,0:T(8,128)(2,1)}, bf16[32,3,16,512]{3,2,1,0:T(8,128)(2,1)}, f32[3,3,8,512]{3,2,1,0:T(8,1...) custom-call(bf16[3,3,512,512]{3,2,1,0:T(8,128)(2,1)} %stream_ref.3, ...), custom_call_target="tpu_custom_call" | custom-call | tf_op jit(solution)/shard_map/front/pallas_call | solution.py:508
  37.1 45.8 %long.1 = (f32[32,3,16,512]{3,2,1,0:T(8,128)}, f32[32,3,16,512]{3,2,1,0:T(8,128)}, f32[32,1,128]{2,1,0:T(1,128)}) custom-call(bf16[32,3,16,512]{3,2,1,0:T(8,128)(2,1)} %get-tuple-element.26.u_ref, bf16[32,3,16,128]{3,2,1,0:T(8,128)(2,1)} %get-tuple-element.27.u_halo_ref, bf16[32,3,16,512]{3,2,1,0:T(8,128)(2,1)} %get-tuple-element.28.e_ref, ...), custom_call_target="tpu_custom_call" | custom-call | tf_op jit(solution)/shard_map/long/pallas_call | solution.py:546
  82.9 18.9 %back.1 = (bf16[3,512,512]{2,1,0:T(8,128)(2,1)}, bf16[3,3,512,512]{3,2,1,0:T(8,128)(2,1)}, bf16[3,3,8,512]{3,2,1,0:T(8,128)(2,1)}, f32[3,3,8,512]{3,2,1,0:T(8,128)}, f32[24,128]{1,0:T(8,128)}) custom-call(f32[3,3,512,512]{3,2,1,0:T(8,128)} %get-tuple-element.23.short_ref, bf16[3,3,512,512]{3,2,1,0:T(8,128)(2,1)} %stream_ref.3, ...), custom_call_target="tpu_custom_call" | custom-call | tf_op jit(solution)/shard_map/back/pallas_call | solution.py:564
  101.8 19.5 %reduce.1 = (f32[3,7,32]{2,1,0:T(8,128)}, f32[32,128]{1,0:T(8,128)}, bf16[3,3,8,512]{3,2,1,0:T(8,128)(2,1)}) custom-call(f32[24,128]{1,0:T(8,128)} %get-tuple-element.36.corr_ref, f32[32,128]{1,0:T(8,128)} %bitcast.4, bf16[3,3,8,512]{3,2,1,0:T(8,128)(2,1)} %get-tuple-element.38.head_ref), custom_call_target="tpu_custom_call" | custom-call | tf_op jit(solution)/shard_map/reduce/pallas_call | solution.py:588
  121.3 0.0 copy-start.1
  121.3 0.0 copy-start
  121.3 1.9 %edge.1 = bf16[3,3,512,512]{3,2,1,0:T(8,128)(2,1)} custom-call(bf16[3,3,512,512]{3,2,1,0:T(8,128)(2,1)} %get-tuple-element.34.grad_ref, f32[3,3,8,512]{3,2,1,0:T(8,128)} %get-tuple-element.35.tail_ref, bf16[3,3,8,512]{3,2,1,0:T(8,128)(2,1)} %get-tuple-element.39.head_ref, f32[3,8,512]{2,1,0:T(8,128)} %get-tuple-element.25.tap_ref), custom_call_target="tpu_custom_call", output_to_operand_aliasing={{}: (0, {})} | custom-call | tf_op jit(solution)/shard_map/edge/pallas_call | solution.py:611
  123.2 0.0 copy-done.1
  123.2 0.6 copy.14
  123.8 0.0 copy-done
  123.8 0.6 copy.15
Async XLA Ops:
  121.3 1.9 %copy-start.1 = (f32[3,7,32]{2,1,0:T(8,128)S(1)}, f32[3,7,32]{2,1,0:T(8,128)}, u32[]{:S(2)}) copy-start(f32[3,7,32]{2,1,0:T(8,128)} %get-tuple-element.48) | copy-start | bytes 8068
  121.3 2.5 %copy-start = (f32[32,128]{1,0:T(8,128)S(1)}, f32[32,128]{1,0:T(8,128)}, u32[]{:S(2)}) copy-start(f32[32,128]{1,0:T(8,128)} %get-tuple-element.41) | copy-start | bytes 49156

commit v3 on v2

--- a/solution.py
+++ b/solution.py
@@ -1,4 +1,5 @@
 import functools
+from itertools import zip_longest
 
 import jax
 import jax.numpy as jnp
@@ -234,6 +235,7 @@
     turned_ref[...] = jnp.concatenate(parts, axis=0).T
     zero = jnp.zeros((LANES, LANES), bf16)
     eye = group_mask((POLES, POLES), 1, 1)
+    batch = 4
 
     def lanes(shape):
         return lax.broadcasted_iota(jnp.int32, shape, 1).astype(f32)
@@ -268,26 +270,32 @@
             high, low = split(value)
             return jnp.concatenate([high, high, low], axis=0)
 
+        yield
         near = jnp.exp(-float(half) * rate_row)
         ahead = ahead - local_state(u_halo, (LANES - 1.0) - edge)
         ahead_columns = columns([ahead, ahead * near])
         far = (behind - local_state(e_halo, edge)) * jnp.exp(float(half) * rate_row)
         behind_columns = columns([behind * near, behind, far])
 
+        yield
         lag = lanes((POLES, 5 * LANES))
         h_row = jnp.sum(residue * jnp.exp(-rate * lag), axis=0, keepdims=True)
         h_tiles, _ = slanted(h_row)
+        yield
         taps = tap_ref[pl.ds(group, 1), :].astype(f32)
         q = matmul(jnp.broadcast_to(taps, (16, LANES)).astype(bf16), jnp.concatenate(h_tiles, axis=1))[:1]
+        yield
         q_tiles, _ = slanted(q)
         k_tiles, k_last = slanted(taps)
         k_tile = k_tiles[0]
 
+        yield
         moment = jnp.sum(taps * jnp.exp(rate * edge), axis=1, keepdims=True)
         time = lanes((POLES, half))
         ahead_weights = weights(residue * moment * jnp.exp(-rate * (time + 1.0)))
         behind_weights = weights(residue * jnp.exp(-rate * (half - time)))
 
+        yield
         left = jnp.concatenate([jnp.concatenate([jnp.zeros((rows, half), bf16), u_ext[:, : 3 * LANES]], axis=1), u_ext], axis=0)
         left_tiles = [zero] + q_tiles
         right = jnp.concatenate(
@@ -296,6 +304,7 @@
         s = matmul(left, right) + matmul(ahead_columns, ahead_weights)
         s_ref[index] = jnp.concatenate([s[:rows], s[rows:]], axis=1).reshape(3, GROUP, length)
 
+        yield
         left = jnp.concatenate(
             [
                 e_own,
@@ -311,6 +320,7 @@
         tail = jnp.where(has_next, p[2 * rows :, :LANES], 0.0)
         p = jnp.concatenate([p[:rows], p[rows : 2 * rows], tail], axis=1).astype(bf16)
 
+        yield
         left = jnp.concatenate([p[:, : 3 * LANES], p[:, half:]], axis=0)
         right = jnp.concatenate(
             [jnp.concatenate([k_tile, k_last, zero], axis=1), jnp.concatenate([zero, k_tile, k_last], axis=1)], axis=0
@@ -318,9 +328,11 @@
         w = matmul(left, right, NT)
         w_ref[index] = jnp.concatenate([w[:rows], w[rows:]], axis=1).reshape(3, GROUP, length)
 
+        yield
         p_stack = jnp.concatenate([p[:, LANES * b : LANES * (b + 1)] for b in range(4)], axis=0)
         u_stack = jnp.concatenate([u_ext[:, LANES * b : LANES * (b + 2)] for b in range(4)], axis=0)
         table = matmul(p_stack.T, u_stack)
+        yield
         total = table[LANES - 8 :]
         for tile in reversed(range(LANES // 8 - 1)):
             total = pltpu.roll(total, 2 * LANES - 8, 1) + table[8 * tile : 8 * tile + 8]
@@ -331,11 +343,11 @@
         lag_ref[index] = pltpu.roll(total, 2 * LANES - 1, 1)[:, :LANES]
 
     def body(step, carry):
-        one(2 * step)
-        one(2 * step + 1)
+        for _ in zip_longest(*[one(batch * step + k) for k in range(batch)]):
+            pass
         return carry
 
-    lax.fori_loop(0, per_step // 2, body, 0)
+    lax.fori_loop(0, per_step // batch, body, 0)
 
 
 def back_kernel(short_ref, stream_ref, prev_ref, tap_ref, cot_ref, s_ref, w_ref, out_ref, grad_ref, head_ref, tail_ref, corr_ref,

time: 125 us -> 107 us (0.86)
  Pallas kernels: 121 us -> 103 us
    pallas_call x1, Pallas kernels: 45.8 us -> 27.7 us  [on_device(): pl.pallas_call(long_kernel, grid=(chunks,), in_specs=[own_spec, halo_spec...]
where the time goes in v3:
time: 107 us; the launch traced here: 106 us
  Pallas kernels  103 us (96%)
  other arithmetic  1.3 us (1%)
  local copies, waits for them, and re-layouts  1.21 us (1%)
    pallas_call x1, Pallas kernels, on_device(): pl.pallas_call(functools.partial(front_kernel, count), grid=(chunks, seqs...  35.2 us
    pallas_call x1, Pallas kernels, on_device(): pl.pallas_call(long_kernel, grid=(chunks,), in_specs=[own_spec, halo_spec...  27.7 us
    pallas_call x1, Pallas kernels, on_device(): pl.pallas_call(functools.partial(reduce_kernel, count, across), in_specs=...  19.5 us
    pallas_call x1, Pallas kernels, on_device(): pl.pallas_call(back_kernel, grid=(chunks, seqs), in_specs=[stream_spec, s...  18.9 us

profile of v3, /device:TPU:1, one launch (start us, length us, event | category | flops | bytes accessed | tf_op | source)
XLA Modules:
  0.0 106.2 jit_solution(9572781693313979943)
XLA Ops:
  0.6 1.3 %convert_bitcast_fusion.tap_ref = f32[32,128]{1,0:T(8,128)} fusion(bf16[128,32]{0,1:T(8,128)(2,1)} %param.8), kind=kLoop, calls=%fused_computation | loop fusion | flops 4096 | bytes 24576 | tf_op jit(solution)/shard_map/transpose | solution.py:574
  1.9 35.2 %front.1 = (f32[3,3,512,512]{3,2,1,0:T(8,128)}, bf16[32,3,16,512]{3,2,1,0:T(8,128)(2,1)}, bf16[32,3,16,512]{3,2,1,0:T(8,128)(2,1)}, f32[3,3,8,512]{3,2,1,0:T(8,1...) custom-call(bf16[3,3,512,512]{3,2,1,0:T(8,128)(2,1)} %stream_ref.3, ...), custom_call_target="tpu_custom_call" | custom-call | tf_op jit(solution)/shard_map/front/pallas_call | solution.py:520
  37.1 27.7 %long.1 = (f32[32,3,16,512]{3,2,1,0:T(8,128)}, f32[32,3,16,512]{3,2,1,0:T(8,128)}, f32[32,1,128]{2,1,0:T(1,128)}) custom-call(bf16[32,3,16,512]{3,2,1,0:T(8,128)(2,1)} %get-tuple-element.26.u_ref, bf16[32,3,16,128]{3,2,1,0:T(8,128)(2,1)} %get-tuple-element.27.u_halo_ref, bf16[32,3,16,512]{3,2,1,0:T(8,128)(2,1)} %get-tuple-element.28.e_ref, ...), custom_call_target="tpu_custom_call" | custom-call | tf_op jit(solution)/shard_map/long/pallas_call | solution.py:558
  64.8 18.9 %back.1 = (bf16[3,512,512]{2,1,0:T(8,128)(2,1)}, bf16[3,3,512,512]{3,2,1,0:T(8,128)(2,1)}, bf16[3,3,8,512]{3,2,1,0:T(8,128)(2,1)}, f32[3,3,8,512]{3,2,1,0:T(8,128)}, f32[24,128]{1,0:T(8,128)}) custom-call(f32[3,3,512,512]{3,2,1,0:T(8,128)} %get-tuple-element.23.short_ref, bf16[3,3,512,512]{3,2,1,0:T(8,128)(2,1)} %stream_ref.3, ...), custom_call_target="tpu_custom_call" | custom-call | tf_op jit(solution)/shard_map/back/pallas_call | solution.py:576
  83.7 19.5 %reduce.1 = (f32[3,7,32]{2,1,0:T(8,128)}, f32[32,128]{1,0:T(8,128)}, bf16[3,3,8,512]{3,2,1,0:T(8,128)(2,1)}) custom-call(f32[24,128]{1,0:T(8,128)} %get-tuple-element.36.corr_ref, f32[32,128]{1,0:T(8,128)} %bitcast.4, bf16[3,3,8,512]{3,2,1,0:T(8,128)(2,1)} %get-tuple-element.38.head_ref), custom_call_target="tpu_custom_call" | custom-call | tf_op jit(solution)/shard_map/reduce/pallas_call | solution.py:600
  103.2 0.0 copy-start.1
  103.2 0.0 copy-start
  103.2 1.9 %edge.1 = bf16[3,3,512,512]{3,2,1,0:T(8,128)(2,1)} custom-call(bf16[3,3,512,512]{3,2,1,0:T(8,128)(2,1)} %get-tuple-element.34.grad_ref, f32[3,3,8,512]{3,2,1,0:T(8,128)} %get-tuple-element.35.tail_ref, bf16[3,3,8,512]{3,2,1,0:T(8,128)(2,1)} %get-tuple-element.39.head_ref, f32[3,8,512]{2,1,0:T(8,128)} %get-tuple-element.25.tap_ref), custom_call_target="tpu_custom_call", output_to_operand_aliasing={{}: (0, {})} | custom-call | tf_op jit(solution)/shard_map/edge/pallas_call | solution.py:623
  105.0 0.0 copy-done.1
  105.0 0.6 copy.14
  105.6 0.0 copy-done
  105.6 0.6 copy.15
Async XLA Ops:
  103.2 1.9 %copy-start.1 = (f32[3,7,32]{2,1,0:T(8,128)S(1)}, f32[3,7,32]{2,1,0:T(8,128)}, u32[]{:S(2)}) copy-start(f32[3,7,32]{2,1,0:T(8,128)} %get-tuple-element.48) | copy-start | bytes 8068
  103.2 2.5 %copy-start = (f32[32,128]{1,0:T(8,128)S(1)}, f32[32,128]{1,0:T(8,128)}, u32[]{:S(2)}) copy-start(f32[32,128]{1,0:T(8,128)} %get-tuple-element.41) | copy-start | bytes 49156
